TPU v7x, 512 devices: a whole 4x8x8 slice. The times are simulated.
512 devices in a mesh: tile: 16 (over z_lo, x, core), kern: 32 (over z_hi, y).
Axes of the slice: x: 4, y: 8, z: 8 (z_hi: 4, z_lo: 2; z = z_hi * 2 + z_lo), core: 2. Of those that a mesh axis runs over, the one named last changes fastest.
Arguments:
- mask: float32 [1024, 2048], P('tile'), may hold values from 0 to 1
- target: int32 [1024, 2048], P('tile'), may hold values 0 or 1
- kernels: bfloat16 [32, 2, 21, 21], P('kern'), may hold values from -0.25 to 0.25
- source_weight: float32 [32], replicated, may hold values from 0.2 to 2
- assign: int32 [32], P('kern'), may hold values from 0 to 31, each once
Outputs:
- mask_grad: float32 [1024, 2048], P('tile', 'kern')
- resist: float32 [1024, 2048], P('tile', 'kern')
Inputs may be any that keep to these rules, and one draw needn't show every extreme that they name: assign is a permutation of 0 to 31.
All inputs are finite; a program needn't handle non-finite values. No bound on the sum of `target` on one device may be relied on, other than what follows from the above.
Results may differ from a plain program's by a relative error of at most 0.0036.
Values may be sent and summed in bfloat16 or wider, within the bound.
No kernel may reach another device: no remote copies, remote signals or barrier semaphores. Data moves between devices by JAX's collectives and lax.ppermute only.
A program may use at most 64 MiB of HBM per device.

v0:
```python
import jax
import jax.numpy as jnp
from jax import lax
from jax.sharding import PartitionSpec as P

SLOPE_FACTOR = 4.0
LEVEL_VALUE = 0.6


def padded_2(cells, sides, width):
    for axis, dim in sides:
        count = lax.axis_size(axis)
        ends = count - 1
        head = lax.slice_in_dim(cells, 0, width, axis=dim)
        tail = lax.slice_in_dim(cells, cells.shape[dim] - width, cells.shape[dim], axis=dim)
        cells = jnp.concatenate(
            [
                lax.ppermute(tail, axis, [(i, (i + 1) % count) for i in range(ends)]),
                cells,
                lax.ppermute(head, axis, [((i + 1) % count, i) for i in range(ends)]),
            ],
            axis=dim,
        )
    return cells


def split_up(array, dim, size):
    shape = array.shape
    blocks = array.reshape(*shape[:dim], size, shape[dim] // size, *shape[dim + 1 :])
    return jnp.moveaxis(blocks, dim, 0)


def sent_and_summed(array, axis, dim):
    blocks = split_up(array, dim, lax.axis_size(axis))
    arrived = lax.all_to_all(blocks, axis, split_axis=0, concat_axis=0, tiled=True)
    return arrived.sum(axis=0)


def in_order(blocks, dim):
    shape = list(blocks.shape[1:])
    shape[dim] *= blocks.shape[0]
    return jnp.moveaxis(blocks, 0, dim).reshape(shape)


def from_everyone(array, axis):
    copies = jnp.broadcast_to(array, (lax.axis_size(axis), *array.shape))
    return lax.all_to_all(copies, axis, split_axis=0, concat_axis=0, tiled=True)


def gather_directly(array, axis, dim):
    return in_order(from_everyone(array, axis), dim)


def windows_of(extended, col_count):
    blocks = col_count // 128
    head_shape = extended.shape[:-1]
    leading = extended[..., :col_count].reshape(head_shape + (blocks, 128))
    trailing = extended[..., 128 : col_count + 128].reshape(head_shape + (blocks, 128))
    return jnp.concatenate([leading, trailing], axis=-1)


def column_windows(padded, margin, col_count):
    widths = [(0, 0)] * (padded.ndim - 1) + [(margin, 256 - margin)]
    return windows_of(jnp.pad(padded, widths), col_count)


def select_table(span_len):
    column = jnp.arange(256)[:, None, None]
    output = jnp.arange(128)[None, :, None]
    tapped = jnp.arange(span_len)[None, None, :]
    return (column - output == tapped).astype(jnp.float32)


def forward_matrix(kernel_pair):
    span_len = kernel_pair.shape[-1]
    matrix = jnp.einsum("tij,coj->icto", kernel_pair.astype(jnp.float32), select_table(span_len))
    return matrix.reshape(span_len, 256, 256).astype(jnp.bfloat16)


def adjoint_matrix(kernel_pair):
    span_len = kernel_pair.shape[-1]
    flipped = kernel_pair[:, ::-1, ::-1]
    matrix = jnp.einsum("tij,coj->itco", flipped.astype(jnp.float32), select_table(span_len))
    return matrix.astype(jnp.bfloat16)


def forward_fields(windows, matrix, out_rows):
    blocks = windows.shape[-2]
    col_count = blocks * 128

    def forward_accumulate(offset, running):
        sliced = lax.dynamic_slice_in_dim(windows, offset, out_rows, 0)
        return running + jnp.einsum(
            "rbc,cn->rbn", sliced, matrix[offset], preferred_element_type=jnp.float32
        )

    running = lax.fori_loop(
        0, matrix.shape[0], forward_accumulate, jnp.zeros((out_rows, blocks, 256), jnp.float32)
    )
    return (
        running[..., :128].reshape(out_rows, col_count),
        running[..., 128:].reshape(out_rows, col_count),
    )


def adjoint_field(windows, matrix, out_rows):
    blocks = windows.shape[-2]
    col_count = blocks * 128

    def adjoint_accumulate(offset, running):
        sliced = lax.dynamic_slice_in_dim(windows, offset, out_rows, 0)
        return running + jnp.einsum(
            "rtbc,tcn->rbn", sliced, matrix[offset], preferred_element_type=jnp.float32
        )

    running = lax.fori_loop(
        0, matrix.shape[0], adjoint_accumulate, jnp.zeros((out_rows, blocks, 128), jnp.float32)
    )
    return running.reshape(out_rows, col_count)


def on_device(mask, target, kernels, source_weight, assign):
    own_rows = mask.shape[0]
    col_count = mask.shape[1]
    span_len = kernels.shape[-1]
    margin = (span_len - 1) // 2
    kern_count = lax.axis_size("kern")
    share = col_count // kern_count
    kern_index = lax.axis_index("kern")
    mask_copy = mask.astype(jnp.bfloat16)
    total = jnp.sum(source_weight)
    slot_ids = jnp.arange(source_weight.shape[0])[None, :]
    picked = (assign[:, None] == slot_ids).astype(jnp.float32)
    local_weight = jnp.sum(picked * source_weight[None, :], axis=1)
    mask_padded = padded_2(mask_copy, (("tile", 0),), margin)
    target_rows = target.astype(jnp.float32)
    inside = jnp.ones((own_rows,), jnp.bool_)
    mask_windows = column_windows(mask_padded, margin, col_count)
    source = 0
    real_part, imag_part = forward_fields(mask_windows, forward_matrix(kernels[source]), own_rows)
    field_list = [(real_part, imag_part)]
    partial_value = local_weight[source] * (real_part * real_part + imag_part * imag_part)
    aerial_share = sent_and_summed(partial_value, "kern", 1) / total
    resist_own = jax.nn.sigmoid(SLOPE_FACTOR * (aerial_share - LEVEL_VALUE))
    target_share = lax.dynamic_slice_in_dim(target_rows, kern_index * share, share, 1)
    sense_share = 2.0 * (resist_own - target_share) * SLOPE_FACTOR * resist_own * (1.0 - resist_own)
    sense = gather_directly(sense_share, "kern", 1)
    sense = jnp.where(inside[:, None], sense, 0.0)
    adjoint_list = []
    source = 0
    factor = 2.0 * local_weight[source] / total
    adjoint_list.append(factor * sense * field_list[source][0])
    adjoint_list.append(factor * sense * field_list[source][1])
    adjoints = jnp.stack(adjoint_list, axis=1).astype(jnp.bfloat16)
    adjoint_padded = padded_2(adjoints, (("tile", 0),), margin)
    source = 0
    grad_terms = adjoint_field(
        column_windows(adjoint_padded, margin, col_count), adjoint_matrix(kernels[source]), own_rows
    )
    mask_grad = sent_and_summed(grad_terms, "kern", 1)
    return (mask_grad, resist_own)


def solution(mesh):
    placed = (P("tile", None), P("tile", None), P("kern", None, None, None), P(), P("kern"))
    return jax.shard_map(
        on_device,
        mesh=mesh,
        in_specs=placed,
        out_specs=(P("tile", "kern"), P("tile", "kern")),
        check_vma=False,
    )
```

profile of v0, /device:TPU:10, one launch (start us, length us, event | category | flops | bytes accessed | tf_op | source)
XLA Modules:
  0.0 193.3 jit_solution(1955887751735547513)
XLA Ops:
  1.7 1.9 collective-permute-start
  3.7 3.6 %collective-permute-start.1 = (bf16[10,2048]{1,0:T(8,128)(2,1)S(1)}, bf16[10,2048]{1,0:T(8,128)(2,1)S(1)}, u32[]{:S(2)}, u32[]{:S(2)}) collective-permute-start(bf16[10,2048]{1,0:T(8,128)(2,1)S(1)} %get-tuple-element.260), channel_id=1, source_target_pairs={{32,0},{64,32},{96,64},{128,96},{160,128},{192,160},{224,192},{256... | collective-permute-start | bytes 122888 | tf_op jit(solution)/shard_map/ppermute | solution.py:20
  8.0 3.4 %convert_bitcast_fusion.1 = bf16[21,256,2,128]{3,0,2,1:T(8,128)(2,1)} fusion(s32[256,128]{1,0:T(8,128)S(1)} %iota_subtract_fusion, bf16[2,21,21]{2,0,1:T(2,128)(2,1)} %bitcast.69), kind=kOutput, calls=%fused_computation.12 | convolution fusion | flops 59867136 | bytes 2885348 | tf_op jit(solution)/shard_map/tij,coj->icto/dot_general | solution.py:76
  12.0 4.9 %copy.37 = bf16[21,256,2,128]{1,3,2,0:T(8,128)(2,1)} copy(bf16[21,256,2,128]{3,0,2,1:T(8,128)(2,1)} %convert_bitcast_fusion.1) | data formatting | bytes 5505024 | tf_op jit(solution)/shard_map/convert_element_type | solution.py:77
  17.5 29.3 %while.28 = (s32[]{:T(128)}, f32[64,16,256]{2,1,0:T(8,128)S(1)}, bf16[84,16,256]{2,1,0:T(8,128)(2,1)S(1)}, bf16[21,256,256]{1,2,0:T(8,128)(2,1)}, s32[]{:T(128)}, /*index=5*/s32[]{:T(128)}) while((s32[]{:T(128)}, f32[64,16,256]{2,1,0:T(8,128)S(1)}, bf16[84,16,256]{2,1,0:T(8,128)(2,1)S(1)}, bf16[21,256,256]{1,2,0:T(8,128)(2,1)}, ...), condition=%wide.region_3.4_spmd.clone, body=%wide.region_2.3_spmd.clone.sunk | while | flops 134742016 | bytes 2753615 | solution.py:97
  48.4 1.4 reshape.110
  49.8 16.2 %all-to-all-start = ((f32[32,1,4096]{2,1,0:T(1,128)}), f32[32,1,4096]{2,1,0:T(1,128)S(1)}, u32[]{:S(2)}, u32[]{:S(2)}) async-start(f32[32,1,4096]{2,1,0:T(1,128)} %reshape.110), calls=%async_computation | async-start | bytes 1048576 | tf_op jit(solution)/shard_map/all_to_all | solution.py:35
  66.0 20.2 %all-to-all-done = f32[32,1,4096]{2,1,0:T(1,128)S(1)} async-done(((f32[32,1,4096]{2,1,0:T(1,128)}), f32[32,1,4096]{2,1,0:T(1,128)S(1)}, u32[]{:S(2)}, u32[]{:S(2)}) %all-to-all-start) | async-done | bytes 524320 | tf_op jit(solution)/shard_map/all_to_all | solution.py:35
  86.8 1.9 %reduce.2 = f32[32,4096]{1,0:T(8,128)S(1)} reduce(f32[32,1,4096]{2,1,0:T(1,128)S(1)} %all-to-all-done, f32[]{:T(128)} %broadcast.113), dimensions={1}, to_apply=%all_to_all.9.reduce_sub_computation | reduce | bytes 1048580 | tf_op jit(solution)/shard_map/all_to_all | solution.py:35
  89.2 2.0 %fusion.33 = (f32[64,64]{1,0:T(8,128)S(1)}, f32[64,64]{1,0:T(8,128)}) fusion(s32[64,2048]{1,0:T(8,128)} %param.10, s32[]{:T(128)S(6)} %select_n.27, f32[64,64]{1,0:T(8,128)S(1)} %reduce_sum.38, f32[]{:T(128)} %get-tuple-element.228), kind=kLoop, calls=%fused_computation.48 | loop fusion | flops 49152 | bytes 65544 | tf_op jit(solution)/shard_map/mul | solution.py:146
  91.3 1.4 reshape.112
  92.8 4.5 %all-to-all-start.1 = ((f32[32,1,4096]{2,1,0:T(1,128)}), f32[32,1,4096]{2,1,0:T(1,128)S(1)}, u32[]{:S(2)}, u32[]{:S(2)}) async-start(f32[32,1,4096]{2,1,0:T(1,128)} %reshape.112), calls=%async_computation.1 | async-start | bytes 1048576 | tf_op jit(solution)/shard_map/all_to_all | solution.py:47
  98.8 18.2 %all-to-all-done.1 = f32[32,1,4096]{2,1,0:T(1,128)S(1)} async-done(((f32[32,1,4096]{2,1,0:T(1,128)}), f32[32,1,4096]{2,1,0:T(1,128)S(1)}, u32[]{:S(2)}, u32[]{:S(2)}) %all-to-all-start.1) | async-done | bytes 524320 | tf_op jit(solution)/shard_map/all_to_all | solution.py:47
  117.0 1.9 %reduce.3 = f32[32,4096]{1,0:T(8,128)S(1)} reduce(f32[32,1,4096]{2,1,0:T(1,128)S(1)} %all-to-all-done.1, f32[]{:T(128)} %broadcast.113), dimensions={1}, to_apply=%all_to_all.10.reduce_sub_computation | reduce | bytes 1048580 | tf_op jit(solution)/shard_map/all_to_all | solution.py:47
  120.6 1.9 collective-permute-start.2
  122.5 3.8 %collective-permute-start.3 = (bf16[10,2,2048]{2,0,1:T(8,128)(2,1)S(1)}, bf16[10,2,2048]{2,0,1:T(8,128)(2,1)S(1)}, u32[]{:S(2)}, u32[]{:S(2)}) collective-permute-start(bf16[10,2,2048]{2,0,1:T(8,128)(2,1)S(1)} %get-tuple-element.254), channel_id=1, source_target_pairs={{32,0},{64,32},{96,64},{128,96},{160,128},{192,160},{224,192},{256... | collective-permute-start | bytes 245768 | tf_op jit(solution)/shard_map/ppermute | solution.py:20
  126.3 2.6 %convert_bitcast_fusion = bf16[21,2,256,128]{3,0,1,2:T(8,128)(2,1)} fusion(s32[256,128]{1,0:T(8,128)S(1)} %iota_subtract_fusion, bf16[2,21,21]{2,0,1:T(2,128)(2,1)S(1)} %rev.3), kind=kOutput, calls=%fused_computation.11 | convolution fusion | flops 59867136 | bytes 2885348 | tf_op jit(solution)/shard_map/tij,coj->itco/dot_general | solution.py:83
  129.0 4.2 %copy.43 = bf16[21,2,256,128]{3,2,1,0:T(8,128)(2,1)} copy(bf16[21,2,256,128]{3,0,1,2:T(8,128)(2,1)} %convert_bitcast_fusion) | data formatting | bytes 5505024
  134.7 29.8 %while.29 = (s32[]{:T(128)}, f32[64,16,128]{2,1,0:T(8,128)S(1)}, bf16[84,2,16,256]{3,2,0,1:T(8,128)(2,1)S(1)}, bf16[21,2,256,128]{3,2,1,0:T(8,128)(2,1)}, s32[]{:T(128)}, /*index=5*/s32[]{:T(128)}) while((s32[]{:T(128)}, f32[64,16,128]{2,1,0:T(8,128)S(1)}, bf16[84,2,16,256]{3,2,0,1:T(8,128)(2,1)S(1)}, ...), condition=%wide.region_6.7_spmd.clone, body=%wide.region_5.6_spmd.clone.sunk | while | flops 134479872 | bytes 2229327 | solution.py:116
  139.0 1.4 fusion.53
  140.4 1.4 fusion.53
  141.8 1.4 fusion.53
  143.2 1.4 fusion.53
  144.7 1.4 fusion.53
  147.5 1.4 fusion.53
  150.3 1.4 fusion.53
  153.2 1.4 fusion.53
  156.0 1.4 fusion.53
  158.8 1.4 fusion.53
  161.7 1.4 fusion.53
  166.0 24.2 %all_to_all.15 = f32[32,1,4096]{2,1,0:T(1,128)S(1)} all-to-all(f32[32,1,4096]{2,1,0:T(1,128)S(1)} %reshape.114), channel_id=1, replica_groups=mesh['tile'=16,'kern'=32] {'kern'}, dimensions={0} | all-to-all | bytes 1048576 | tf_op jit(solution)/shard_map/all_to_all | solution.py:35
  190.2 1.9 %reduce.4 = f32[32,4096]{1,0:T(8,128)S(1)} reduce(f32[32,1,4096]{2,1,0:T(1,128)S(1)} %all_to_all.15, f32[]{:T(128)} %broadcast.113), dimensions={1}, to_apply=%all_to_all.11.reduce_sub_computation | reduce | bytes 1048580 | tf_op jit(solution)/shard_map/all_to_all | solution.py:35
  (78 shorter events, 53.7 us)
Async XLA Ops:
  1.7 15.2 %collective-permute-start = (bf16[10,2048]{1,0:T(8,128)(2,1)S(1)}, bf16[10,2048]{1,0:T(8,128)(2,1)S(1)}, u32[]{:S(2)}, u32[]{:S(2)}) collective-permute-start(bf16[10,2048]{1,0:T(8,128)(2,1)S(1)} %get-tuple-element.259), channel_id=1, source_target_pairs={{0,32},{32,64},{64,96},{96,128},{128,160},{160,192},{192,224},{224... | collective-permute-start | bytes 122888 | tf_op jit(solution)/shard_map/ppermute | solution.py:18
  3.7 13.2 %collective-permute-start.1 = (bf16[10,2048]{1,0:T(8,128)(2,1)S(1)}, bf16[10,2048]{1,0:T(8,128)(2,1)S(1)}, u32[]{:S(2)}, u32[]{:S(2)}) collective-permute-start(bf16[10,2048]{1,0:T(8,128)(2,1)S(1)} %get-tuple-element.260), channel_id=1, source_target_pairs={{32,0},{64,32},{96,64},{128,96},{160,128},{192,160},{224,192},{256... | collective-permute-start | bytes 122888 | tf_op jit(solution)/shard_map/ppermute | solution.py:20
  8.0 3.4 %copy-start.1 = (f32[32]{0:T(128)S(1)}, f32[32]{0:T(128)}, u32[]{:S(2)}) copy-start(f32[32]{0:T(128)} %param.12) | copy-start | bytes 388
  49.8 36.3 %all-to-all-start = ((f32[32,1,4096]{2,1,0:T(1,128)}), f32[32,1,4096]{2,1,0:T(1,128)S(1)}, u32[]{:S(2)}, u32[]{:S(2)}) async-start(f32[32,1,4096]{2,1,0:T(1,128)} %reshape.110), calls=%async_computation | async-start | bytes 1048576 | tf_op jit(solution)/shard_map/all_to_all | solution.py:35
  91.2 6.1 %copy-start = (bf16[1,2,21,21]{3,1,2,0:T(2,128)(2,1)S(1)}, bf16[1,2,21,21]{3,1,2,0:T(2,128)(2,1)}, u32[]{:S(2)}) copy-start(bf16[1,2,21,21]{3,1,2,0:T(2,128)(2,1)} %param.11) | copy-start | bytes 5296
  92.8 24.2 %all-to-all-start.1 = ((f32[32,1,4096]{2,1,0:T(1,128)}), f32[32,1,4096]{2,1,0:T(1,128)S(1)}, u32[]{:S(2)}, u32[]{:S(2)}) async-start(f32[32,1,4096]{2,1,0:T(1,128)} %reshape.112), calls=%async_computation.1 | async-start | bytes 1048576 | tf_op jit(solution)/shard_map/all_to_all | solution.py:47
  120.6 12.6 %collective-permute-start.2 = (bf16[10,2,2048]{2,0,1:T(8,128)(2,1)S(1)}, bf16[10,2,2048]{2,0,1:T(8,128)(2,1)S(1)}, u32[]{:S(2)}, u32[]{:S(2)}) collective-permute-start(bf16[10,2,2048]{2,0,1:T(8,128)(2,1)S(1)} %get-tuple-element.253), channel_id=1, source_target_pairs={{0,32},{32,64},{64,96},{96,128},{128,160},{160,192},{192,224},{224... | collective-permute-start | bytes 245768 | tf_op jit(solution)/shard_map/ppermute | solution.py:18
  122.5 10.7 %collective-permute-start.3 = (bf16[10,2,2048]{2,0,1:T(8,128)(2,1)S(1)}, bf16[10,2,2048]{2,0,1:T(8,128)(2,1)S(1)}, u32[]{:S(2)}, u32[]{:S(2)}) collective-permute-start(bf16[10,2,2048]{2,0,1:T(8,128)(2,1)S(1)} %get-tuple-element.254), channel_id=1, source_target_pairs={{32,0},{64,32},{96,64},{128,96},{160,128},{192,160},{224,192},{256... | collective-permute-start | bytes 245768 | tf_op jit(solution)/shard_map/ppermute | solution.py:20
where the time goes:
time: 195 us; the launch traced here: 193 us
  matrix products  64.2 us (33%)
  waiting for transfers between devices  38.4 us (20%)
  starting transfers between devices  32 us (16%)
  blocking collectives  24.2 us (12%)
  local copies, waits for them, and re-layouts  18.6 us (10%)
  other arithmetic  12.1 us (6%)
  between operations  2.82 us (1%)
    dot_general x21, matrix products, adjoint_accumulate(): jnp.einsum('rtbc,tcn->rbn', sliced, matrix[offset], preferred_element_typ...  29.3 us
    dot_general x21, matrix products, forward_accumulate(): jnp.einsum('rbc,cn->rbn', sliced, matrix[offset], preferred_element_type=...  28.8 us
    all_to_all x1, blocking collectives, sent_and_summed(): lax.all_to_all(blocks, axis, split_axis=0, concat_axis=0, tiled=True)  24.2 us
    all_to_all x1, waiting for transfers between devices, sent_and_summed(): lax.all_to_all(blocks, axis, split_axis=0, concat_axis=0, tiled=True)  20.2 us
    all_to_all x1, waiting for transfers between devices, from_everyone(): return lax.all_to_all(copies, axis, split_axis=0, concat_axis=0, tiled=True)  18.2 us
    all_to_all x1, starting transfers between devices, sent_and_summed(): lax.all_to_all(blocks, axis, split_axis=0, concat_axis=0, tiled=True)  16.2 us
    unnamed x13, local copies, waits for them, and re-layouts  9.08 us
    ppermute x2, starting transfers between devices, padded_2(): lax.ppermute(head, axis, [((i + 1) % count, i) for i in range(ends)])  7.46 us
  transfers between devices with their start and end apart: 6, of which 2 were waited for; matrix products, arithmetic and copies ran while one was open for 8% of the time, Pallas kernels for 0%

commit v1 on v0

v1 whole, which is shorter than its diff:
```python
import jax
import jax.numpy as jnp
from jax import lax
from jax.experimental import pallas as pl
from jax.experimental.pallas import tpu as pltpu
from jax.sharding import PartitionSpec as P

OWN = 64
SPAN = 21
HALF = 10
SOURCES = 32
CHANNELS = 2 * SOURCES
DEPTH = 24
TAPS = 512
WEIGHT_SLOT = SPAN * DEPTH
CHUNKS = 11
SLOPE = 4.0
LEVEL = 0.6
VMEM = pltpu.VMEM


def pack_kernel(assign_ref, taps_ref, weight_ref, out_ref):
    slot = lax.broadcasted_iota(jnp.int32, (SPAN, TAPS), 1)
    row = lax.broadcasted_iota(jnp.int32, (SPAN, TAPS), 0)
    low = DEPTH * row
    spread = ((slot >= low) & (slot < low + DEPTH)).astype(jnp.float32).astype(jnp.bfloat16)
    place = slot.astype(jnp.float32)
    inner = place - DEPTH * jnp.floor((place + 0.5) * (1.0 / DEPTH))
    keep = inner == row.astype(jnp.float32)
    index = lax.broadcasted_iota(jnp.int32, (1, SOURCES), 1)
    weight = jnp.sum(jnp.where(index == assign_ref[0], weight_ref[...], 0.0), axis=1, keepdims=True)
    lane = lax.broadcasted_iota(jnp.int32, (1, TAPS), 1)
    rows = []
    for part in range(2):
        wide = jnp.dot(taps_ref[part], spread, preferred_element_type=jnp.float32)
        flat = jnp.sum(jnp.where(keep, wide, 0.0), axis=0, keepdims=True)
        flat = jnp.where(lane == WEIGHT_SLOT, weight, flat)
        rows += [flat[:, 128 * q : 128 * q + 128] for q in range(4)]
    out_ref[...] = jnp.broadcast_to(jnp.concatenate(rows, axis=0)[None], out_ref.shape)


def pack(assign, kernels, source_weight):
    return pl.pallas_call(
        pack_kernel,
        out_shape=jax.ShapeDtypeStruct((SOURCES, 8, 128), jnp.float32),
        in_specs=[
            pl.BlockSpec(memory_space=pltpu.SMEM),
            pl.BlockSpec(memory_space=VMEM),
            pl.BlockSpec(memory_space=VMEM),
        ],
        out_specs=pl.BlockSpec(memory_space=VMEM),
        name="pack",
    )(assign, kernels.reshape(2, SPAN, SPAN), source_weight.reshape(1, SOURCES))


def window_kernel(ids_ref, mask_a, mask_b, target_a, target_b, own_ref, up_ref, down_ref):
    kern = ids_ref[1]
    odd = lax.rem(kern, 2) == 1

    def cut(left, right, even_start, odd_start):
        left = jnp.where(kern > 0, left, 0.0)
        right = jnp.where(kern < SOURCES - 1, right, 0.0)
        both = jnp.concatenate([left, right], axis=1)
        even = pltpu.roll(both, 256 - even_start, 1)[:, :128]
        other = pltpu.roll(both, 256 - odd_start, 1)[:, :128]
        return jnp.where(odd, other, even).astype(jnp.bfloat16)

    mask = cut(mask_a[...], mask_b[...], 108, 44)
    target = cut(target_a[...].astype(jnp.float32), target_b[...].astype(jnp.float32), 118, 54)
    own_ref[0:64, :] = mask
    own_ref[64:128, :] = target
    up_ref[0:32, :] = mask[0:32]
    up_ref[32:48, :] = target[0:16]
    down_ref[0:32, :] = mask[32:64]
    down_ref[32:48, :] = target[48:64]


def window(ids, mask, target):
    last = mask.shape[1] // 128 - 1

    def left(step, ids):
        return (0, jnp.maximum(lax.div(ids[1] + 1, 2) - 1, 0))

    def right(step, ids):
        return (0, jnp.minimum(lax.div(ids[1] + 1, 2), last))

    return pl.pallas_call(
        window_kernel,
        grid_spec=pltpu.PrefetchScalarGridSpec(
            num_scalar_prefetch=1,
            grid=(1,),
            in_specs=[
                pl.BlockSpec((OWN, 128), left),
                pl.BlockSpec((OWN, 128), right),
                pl.BlockSpec((OWN, 128), left),
                pl.BlockSpec((OWN, 128), right),
            ],
            out_specs=[
                pl.BlockSpec((128, 128), lambda step, ids: (0, 0)),
                pl.BlockSpec((48, 128), lambda step, ids: (0, 0)),
                pl.BlockSpec((48, 128), lambda step, ids: (0, 0)),
            ],
        ),
        out_shape=[
            jax.ShapeDtypeStruct((128, 128), jnp.bfloat16),
            jax.ShapeDtypeStruct((48, 128), jnp.bfloat16),
            jax.ShapeDtypeStruct((48, 128), jnp.bfloat16),
        ],
        name="window",
    )(ids, mask, mask, target, target)


def columns_kernel(ids_ref, own_ref, before_ref, after_ref, cols_ref, aux_ref, side, rows):
    f32 = jnp.float32
    side[0:48, :] = before_ref[...].astype(f32)
    side[48:96, :] = after_ref[...].astype(f32)
    rows[0:20, :] = side[12:32, :]
    rows[20:84, :] = own_ref[0:64, :].astype(f32)
    rows[84:104, :] = side[48:68, :]
    rows[104:112, :] = jnp.zeros((8, 128), f32)
    aux_ref[0, 0:10, :] = side[38:48, :]
    aux_ref[0, 10:74, :] = own_ref[64:128, :].astype(f32)
    aux_ref[0, 74:84, :] = side[80:90, :]
    aux_ref[0, 84:88, :] = jnp.zeros((4, 128), f32)
    row = lax.broadcasted_iota(jnp.int32, (88, 128), 0) + (OWN * ids_ref[0] - HALF)
    col = lax.broadcasted_iota(jnp.int32, (88, 128), 1) + (OWN * ids_ref[1] - HALF)
    inside = (row >= 0) & (row < ids_ref[2]) & (col >= 0) & (col < ids_ref[3])
    aux_ref[1, :, :] = jnp.where(inside, 2.0 * SLOPE, 0.0)
    base = [rows[0:104, :], rows[4:108, :]]
    for first in range(0, SPAN, 2):
        turned = []
        for tap in (first, first + 1):
            if tap >= SPAN:
                turned.append(None)
            else:
                turned.append([pltpu.roll(b, 128 - tap, 1) if tap else b for b in base])
        for group in range(2 * CHUNKS):
            at = 8 * (group // 2)
            one = turned[0][group % 2][at : at + 24]
            if turned[1] is None:
                two = jnp.zeros((8, 128), f32)
            else:
                two = turned[1][group % 2][at : at + 24]
            block = jnp.concatenate([one, two], axis=0).astype(jnp.bfloat16)
            cols_ref[DEPTH * first : DEPTH * first + block.shape[0], 128 * group : 128 * group + 128] = block


def columns(ids, own, before, after):
    return pl.pallas_call(
        columns_kernel,
        out_shape=[
            jax.ShapeDtypeStruct((TAPS, 256 * CHUNKS), jnp.bfloat16),
            jax.ShapeDtypeStruct((2, 88, 128), jnp.float32),
        ],
        in_specs=[pl.BlockSpec(memory_space=pltpu.SMEM)] + [pl.BlockSpec(memory_space=VMEM)] * 3,
        out_specs=[pl.BlockSpec(memory_space=VMEM)] * 2,
        scratch_shapes=[VMEM((96, 128), jnp.float32), VMEM((112, 128), jnp.float32)],
        name="columns",
    )(ids, own, before, after)


def image_kernel(weight_ref, taps_ref, cols_ref, aux_ref, grad_ref, resist_ref, matrix, sums, seen, final):
    f32 = jnp.float32
    base = jnp.concatenate([taps_ref[pl.ds(q, CHANNELS, stride=4), :] for q in range(4)], axis=1)
    weight = base[:, WEIGHT_SLOT : WEIGHT_SLOT + 1]
    for p in range(4):
        moved = pltpu.roll(base, p, 1) if p else base
        matrix[CHANNELS * p : CHANNELS * (p + 1), :] = moved.astype(jnp.bfloat16)
    total = jnp.sum(weight_ref[...], axis=1, keepdims=True)
    inverse = 1.0 / total
    factor = 2.0 * weight * inverse
    for n in range(CHUNKS):
        fields = jnp.dot(matrix[...], cols_ref[:, 256 * n : 256 * n + 256], preferred_element_type=f32)
        parts = []
        for p in range(4):
            field = fields[CHANNELS * p : CHANNELS * (p + 1)]
            aerial = jnp.sum(weight * (field * field), axis=0, keepdims=True) * inverse
            resist = jax.nn.sigmoid(SLOPE * (aerial - LEVEL))
            low, high = 8 * n + p, 8 * n + 4 + p
            target = jnp.concatenate([aux_ref[0, low : low + 1, :], aux_ref[0, high : high + 1, :]], axis=1)
            scale = jnp.concatenate([aux_ref[1, low : low + 1, :], aux_ref[1, high : high + 1, :]], axis=1)
            sense = scale * (resist - target) * resist * (1.0 - resist)
            seen[low : low + 1, :] = resist[:, :128]
            seen[high : high + 1, :] = resist[:, 128:]
            parts.append(((factor * sense) * field).astype(jnp.bfloat16))
        adjoint = jnp.concatenate(parts, axis=0)
        spread = lax.dot_general(matrix[...], adjoint, (((0,), (0,)), ((), ())), preferred_element_type=f32)
        for tap in range(SPAN):
            for third in range(3):
                tile = n + third
                for parity in range(2):
                    if not 2 <= tile <= 10 - parity:
                        continue
                    at = DEPTH * tap + 8 * third
                    piece = spread[at : at + 8, 128 * parity : 128 * parity + 128]
                    spot = 8 * (tile - 2)
                    if third == 2:
                        sums[parity, tap, spot : spot + 8, :] = piece
                    else:
                        sums[parity, tap, spot : spot + 8, :] += piece
    even = sums[0, 0, :, :]
    odd = sums[1, 0, 0:64, :]
    for tap in range(1, SPAN):
        even = even + pltpu.roll(sums[0, tap, :, :], tap, 1)
        odd = odd + pltpu.roll(sums[1, tap, 0:64, :], tap, 1)
    final[...] = even
    grad = final[4:68, :] + odd
    grad_ref[...] = pltpu.roll(grad, 108, 1)[:, :OWN]
    resist_ref[...] = pltpu.roll(seen[10:74, :], 118, 1)[:, :OWN]


def image(source_weight, taps, cols, aux):
    flops = 2 * 2 * 4 * CHANNELS * TAPS * 256 * CHUNKS
    return pl.pallas_call(
        image_kernel,
        out_shape=[
            jax.ShapeDtypeStruct((OWN, OWN), jnp.float32),
            jax.ShapeDtypeStruct((OWN, OWN), jnp.float32),
        ],
        in_specs=[pl.BlockSpec(memory_space=VMEM)] * 4,
        out_specs=[pl.BlockSpec(memory_space=VMEM)] * 2,
        scratch_shapes=[
            VMEM((4 * CHANNELS, TAPS), jnp.bfloat16),
            VMEM((2, SPAN, 72, 128), jnp.float32),
            VMEM((88, 128), jnp.float32),
            VMEM((72, 128), jnp.float32),
        ],
        cost_estimate=pl.CostEstimate(flops=flops, bytes_accessed=4 << 20, transcendentals=0),
        name="image",
    )(source_weight.reshape(1, SOURCES), taps, cols, aux)


def on_device(mask, target, kernels, source_weight, assign):
    tiles = lax.axis_size("tile")
    tile, kern = lax.axis_index("tile"), lax.axis_index("kern")
    ids = jnp.stack([tile, kern, tiles * mask.shape[0], mask.shape[1]]).astype(jnp.int32)
    taps = lax.all_to_all(pack(assign, kernels, source_weight), "kern", split_axis=0, concat_axis=0, tiled=True)
    own, up, down = window(ids, mask, target)
    before = lax.ppermute(down, "tile", [(i, i + 1) for i in range(tiles - 1)])
    after = lax.ppermute(up, "tile", [(i + 1, i) for i in range(tiles - 1)])
    cols, aux = columns(ids, own, before, after)
    grad, resist = image(source_weight, taps.reshape(SOURCES * 8, 128), cols, aux)
    return (grad, resist)


def solution(mesh):
    placed = (P("tile", None), P("tile", None), P("kern", None, None, None), P(), P("kern"))
    return jax.shard_map(
        on_device,
        mesh=mesh,
        in_specs=placed,
        out_specs=(P("tile", "kern"), P("tile", "kern")),
        check_vma=False,
    )
```

time: 195 us -> 43.3 us (0.22)
  the two profiles are of different devices: /device:TPU:10 before, /device:TPU:15 now
where the time goes in v1:
time: 43.3 us; the launch traced here: 42.8 us
  starting transfers between devices  21.7 us (50%)
  Pallas kernels  11.3 us (26%)
  waiting for transfers between devices  5.39 us (12%)
  local copies, waits for them, and re-layouts  2.57 us (6%)
  between operations  1.33 us (3%)
  other arithmetic  0.59 us (1%)
    all_to_all x1, starting transfers between devices, on_device(): lax.all_to_all(pack(assign, kernels, source_weight), 'kern', split_axis=0...  15.6 us
    ppermute x1, waiting for transfers between devices, on_device(): after = lax.ppermute(up, 'tile', [(i + 1, i) for i in range(tiles - 1)])  5.39 us
    pallas_call x1, Pallas kernels, image(): pl.pallas_call(image_kernel, out_shape=[jax.ShapeDtypeStruct((OWN, OWN),...  4.69 us
    ppermute x1, starting transfers between devices, on_device(): before = lax.ppermute(down, 'tile', [(i, i + 1) for i in range(tiles - 1)])  4.12 us
    pallas_call x1, Pallas kernels, columns(): pl.pallas_call(columns_kernel, out_shape=[jax.ShapeDtypeStruct((TAPS, 256...  2.84 us
    unnamed x7, local copies, waits for them, and re-layouts  2.57 us
    pallas_call x1, Pallas kernels, window(): pl.pallas_call(window_kernel, grid_spec=pltpu.PrefetchScalarGridSpec(num_...  2.21 us
    ppermute x1, starting transfers between devices, on_device(): after = lax.ppermute(up, 'tile', [(i + 1, i) for i in range(tiles - 1)])  1.92 us
  transfers between devices with their start and end apart: 3, of which 1 were waited for; matrix products, arithmetic and copies ran while one was open for 1% of the time, Pallas kernels for 12%

profile of v1, /device:TPU:15, one launch (start us, length us, event | category | flops | bytes accessed | tf_op | source)
XLA Modules:
  0.0 42.8 jit_solution(8191219396760270248)
XLA Ops:
  1.3 1.3 %copy.9 = bf16[1,2,21,21]{3,2,1,0:T(8,128)(2,1)} copy(bf16[1,2,21,21]{3,1,2,0:T(2,128)(2,1)} %param.7) | data formatting | bytes 3528 | tf_op args[2]
  2.6 1.5 %pack.1 = f32[32,8,128]{2,1,0:T(8,128)} custom-call(s32[1]{0:T(128)S(6)} %copy.10.assign_ref, bf16[2,21,21]{2,1,0:T(8,128)(2,1)} %bitcast.8, f32[1,32]{1,0:T(1,128)} %bitcast.9), custom_call_target="tpu_custom_call" | custom-call | tf_op jit(solution)/shard_map/pack/pallas_call | solution.py:43
  4.1 15.6 %all-to-all-start = ((f32[32,8,128]{2,1,0:T(8,128)}), f32[32,8,128]{2,1,0:T(8,128)S(1)}, u32[]{:S(2)}, u32[]{:S(2)}) async-start(f32[32,8,128]{2,1,0:T(8,128)} %pack.1), calls=%async_computation | async-start | bytes 262144 | tf_op jit(solution)/shard_map/all_to_all | solution.py:237
  19.8 0.6 %pad_add_fusion.ids_ref = s32[4]{0:T(128)} fusion(s32[1]{0:T(128)} %constant.12.clone.1, s32[1]{0:T(128)} %constant.11.clone.1, s32[1]{0:T(128)} %bitcast.4, s32[1]{0:T(128)} %bitcast.3), kind=kLoop, calls=%fused_computation.1 | loop fusion | flops 12 | bytes 32 | tf_op jit(solution)/shard_map/stack | solution.py:236
  20.3 2.2 %window.1 = (bf16[128,128]{1,0:T(8,128)(2,1)}, bf16[48,128]{1,0:T(8,128)(2,1)}, bf16[48,128]{1,0:T(8,128)(2,1)}) custom-call(s32[4]{0:T(128)} %pad_add_fusion.ids_ref, f32[64,2048]{1,0:T(8,128)} %mask_b.1, f32[64,2048]{1,0:T(8,128)} %mask_b.1, s32[64,2048]{1,0:T(8,128)} %target_b.1, s32[64,2048]{1,0:T(8,128)} %target_b.1), custom_call_target="tpu_custom_call" | custom-call | tf_op jit(solution)/shard_map/window/pallas_call | solution.py:87
  22.6 4.1 %collective-permute-start = (bf16[48,128]{1,0:T(8,128)(2,1)}, bf16[48,128]{1,0:T(8,128)(2,1)S(1)}, u32[]{:S(2)}, u32[]{:S(2)}) collective-permute-start(bf16[48,128]{1,0:T(8,128)(2,1)} %get-tuple-element.8), channel_id=1, source_target_pairs={{0,32},{32,64},{64,96},{96,128},{128,160},{160,192},{192,224},{224... | collective-permute-start | bytes 36872 | tf_op jit(solution)/shard_map/ppermute | solution.py:239
  26.7 1.9 %collective-permute-start.1 = (bf16[48,128]{1,0:T(8,128)(2,1)}, bf16[48,128]{1,0:T(8,128)(2,1)S(1)}, u32[]{:S(2)}, u32[]{:S(2)}) collective-permute-start(bf16[48,128]{1,0:T(8,128)(2,1)} %get-tuple-element.9), channel_id=1, source_target_pairs={{32,0},{64,32},{96,64},{128,96},{160,128},{192,160},{224,192},{256... | collective-permute-start | bytes 36872 | tf_op jit(solution)/shard_map/ppermute | solution.py:240
  28.6 0.0 collective-permute-done.before_ref
  28.6 0.0 copy-start.1
  28.6 5.4 %collective-permute-done.1.after_ref = bf16[48,128]{1,0:T(8,128)(2,1)S(1)} collective-permute-done((bf16[48,128]{1,0:T(8,128)(2,1)}, bf16[48,128]{1,0:T(8,128)(2,1)S(1)}, u32[]{:S(2)}, u32[]{:S(2)}) %collective-permute-start.1) | collective-permute-done | bytes 12320 | tf_op jit(solution)/shard_map/ppermute | solution.py:240
  34.0 0.0 copy-start.2
  34.0 0.0 copy-done.1
  34.0 0.6 %copy-done.2 = bf16[48,128]{1,0:T(8,128)(2,1)} copy-done((bf16[48,128]{1,0:T(8,128)(2,1)}, bf16[48,128]{1,0:T(8,128)(2,1)S(1)}, u32[]{:S(2)}) %copy-start.2) | copy-done | bytes 12312
  34.6 2.8 %columns.1 = (bf16[512,2816]{1,0:T(8,128)(2,1)}, f32[2,88,128]{2,1,0:T(8,128)}) custom-call(s32[4]{0:T(128)} %pad_add_fusion.ids_ref, bf16[128,128]{1,0:T(8,128)(2,1)} %get-tuple-element.7.own_ref, bf16[48,128]{1,0:T(8,128)(2,1)} %copy-done.1, bf16[48,128]{1,0:T(8,128)(2,1)} %copy-done.2), custom_call_target="tpu_custom_call" | custom-call | tf_op jit(solution)/shard_map/columns/pallas_call | solution.py:149
  37.5 0.0 all-to-all-done
  37.5 0.0 copy-start
  37.5 0.7 %copy-done = f32[32,8,128]{2,1,0:T(8,128)} copy-done((f32[32,8,128]{2,1,0:T(8,128)}, f32[32,8,128]{2,1,0:T(8,128)S(1)}, u32[]{:S(2)}) %copy-start) | copy-done | bytes 131096
  38.1 4.7 %image.1 = (f32[64,64]{1,0:T(8,128)}, f32[64,64]{1,0:T(8,128)}) custom-call(f32[1,32]{1,0:T(1,128)} %bitcast.10, f32[256,128]{1,0:T(8,128)} %bitcast.7, bf16[512,2816]{1,0:T(8,128)(2,1)} %get-tuple-element.10.cols_ref, f32[2,88,128]{2,1,0:T(8,128)} %get-tuple-element.11.aux_ref), custom_call_target="tpu_custom_call" | custom-call | flops 1476395008 | bytes 4194304 | tf_op jit(solution)/shard_map/image/pallas_call | solution.py:214
Async XLA Ops:
  4.1 33.3 %all-to-all-start = ((f32[32,8,128]{2,1,0:T(8,128)}), f32[32,8,128]{2,1,0:T(8,128)S(1)}, u32[]{:S(2)}, u32[]{:S(2)}) async-start(f32[32,8,128]{2,1,0:T(8,128)} %pack.1), calls=%async_computation | async-start | bytes 262144 | tf_op jit(solution)/shard_map/all_to_all | solution.py:237
  22.6 6.1 %collective-permute-start = (bf16[48,128]{1,0:T(8,128)(2,1)}, bf16[48,128]{1,0:T(8,128)(2,1)S(1)}, u32[]{:S(2)}, u32[]{:S(2)}) collective-permute-start(bf16[48,128]{1,0:T(8,128)(2,1)} %get-tuple-element.8), channel_id=1, source_target_pairs={{0,32},{32,64},{64,96},{96,128},{128,160},{160,192},{192,224},{224... | collective-permute-start | bytes 36872 | tf_op jit(solution)/shard_map/ppermute | solution.py:239
  26.7 7.3 %collective-permute-start.1 = (bf16[48,128]{1,0:T(8,128)(2,1)}, bf16[48,128]{1,0:T(8,128)(2,1)S(1)}, u32[]{:S(2)}, u32[]{:S(2)}) collective-permute-start(bf16[48,128]{1,0:T(8,128)(2,1)} %get-tuple-element.9), channel_id=1, source_target_pairs={{32,0},{64,32},{96,64},{128,96},{160,128},{192,160},{224,192},{256... | collective-permute-start | bytes 36872 | tf_op jit(solution)/shard_map/ppermute | solution.py:240
  28.6 5.4 %copy-start.1 = (bf16[48,128]{1,0:T(8,128)(2,1)}, bf16[48,128]{1,0:T(8,128)(2,1)S(1)}, u32[]{:S(2)}) copy-start(bf16[48,128]{1,0:T(8,128)(2,1)S(1)} %collective-permute-done.before_ref) | copy-start | bytes 36868
  34.0 0.6 %copy-start.2 = (bf16[48,128]{1,0:T(8,128)(2,1)}, bf16[48,128]{1,0:T(8,128)(2,1)S(1)}, u32[]{:S(2)}) copy-start(bf16[48,128]{1,0:T(8,128)(2,1)S(1)} %collective-permute-done.1.after_ref) | copy-start | bytes 36868
  37.5 0.7 %copy-start = (f32[32,8,128]{2,1,0:T(8,128)}, f32[32,8,128]{2,1,0:T(8,128)S(1)}, u32[]{:S(2)}) copy-start(f32[32,8,128]{2,1,0:T(8,128)S(1)} %all-to-all-done) | copy-start | bytes 393220

commit v2 on v1

--- a/solution.py
+++ b/solution.py
@@ -10,52 +10,47 @@
 HALF = 10
 SOURCES = 32
 CHANNELS = 2 * SOURCES
+TILES = 16
 DEPTH = 24
 TAPS = 512
 WEIGHT_SLOT = SPAN * DEPTH
+TOTAL_SLOT = WEIGHT_SLOT + 1
 CHUNKS = 11
 SLOPE = 4.0
 LEVEL = 0.6
 VMEM = pltpu.VMEM
 
 
-def pack_kernel(assign_ref, taps_ref, weight_ref, out_ref):
-    slot = lax.broadcasted_iota(jnp.int32, (SPAN, TAPS), 1)
-    row = lax.broadcasted_iota(jnp.int32, (SPAN, TAPS), 0)
-    low = DEPTH * row
+def in_hbm(array):
+    return pltpu.with_memory_space_constraint(array, pltpu.HBM)
+
+
+def prepare_kernel(
+    kern_ref, assign_ref, taps_ref, weight_ref, mask_a, mask_b, target_a, target_b, pack_ref, own_ref, up_ref, down_ref, flat_ref
+):
+    kern = kern_ref[0]
+    odd = lax.rem(kern, 2) == 1
+    flat_ref[...] = jnp.zeros_like(flat_ref)
+    for i in range(SPAN):
+        flat_ref[2 * i : 2 * i + 2, 0:SPAN] = taps_ref[i].astype(jnp.float32)
+    slot = lax.broadcasted_iota(jnp.int32, (128, TAPS), 1)
+    low = DEPTH * lax.broadcasted_iota(jnp.int32, (128, TAPS), 0)
     spread = ((slot >= low) & (slot < low + DEPTH)).astype(jnp.float32).astype(jnp.bfloat16)
-    place = slot.astype(jnp.float32)
+    wide = jnp.dot(flat_ref[...].astype(jnp.bfloat16), spread, preferred_element_type=jnp.float32)
+    place = lax.broadcasted_iota(jnp.int32, wide.shape, 1).astype(jnp.float32)
     inner = place - DEPTH * jnp.floor((place + 0.5) * (1.0 / DEPTH))
-    keep = inner == row.astype(jnp.float32)
+    twice = 2.0 * inner
+    row = lax.broadcasted_iota(jnp.int32, wide.shape, 0).astype(jnp.float32)
     index = lax.broadcasted_iota(jnp.int32, (1, SOURCES), 1)
-    weight = jnp.sum(jnp.where(index == assign_ref[0], weight_ref[...], 0.0), axis=1, keepdims=True)
+    weight = jnp.sum(jnp.where(index == assign_ref[...], weight_ref[...], 0.0), axis=1, keepdims=True)
+    total = jnp.sum(weight_ref[...], axis=1, keepdims=True)
     lane = lax.broadcasted_iota(jnp.int32, (1, TAPS), 1)
     rows = []
     for part in range(2):
-        wide = jnp.dot(taps_ref[part], spread, preferred_element_type=jnp.float32)
-        flat = jnp.sum(jnp.where(keep, wide, 0.0), axis=0, keepdims=True)
-        flat = jnp.where(lane == WEIGHT_SLOT, weight, flat)
+        flat = jnp.sum(jnp.where(row == twice + part, wide, 0.0), axis=0, keepdims=True)
+        flat = jnp.where(lane == WEIGHT_SLOT, weight, jnp.where(lane == TOTAL_SLOT, total, flat))
         rows += [flat[:, 128 * q : 128 * q + 128] for q in range(4)]
-    out_ref[...] = jnp.broadcast_to(jnp.concatenate(rows, axis=0)[None], out_ref.shape)
-
-
-def pack(assign, kernels, source_weight):
-    return pl.pallas_call(
-        pack_kernel,
-        out_shape=jax.ShapeDtypeStruct((SOURCES, 8, 128), jnp.float32),
-        in_specs=[
-            pl.BlockSpec(memory_space=pltpu.SMEM),
-            pl.BlockSpec(memory_space=VMEM),
-            pl.BlockSpec(memory_space=VMEM),
-        ],
-        out_specs=pl.BlockSpec(memory_space=VMEM),
-        name="pack",
-    )(assign, kernels.reshape(2, SPAN, SPAN), source_weight.reshape(1, SOURCES))
-
-
-def window_kernel(ids_ref, mask_a, mask_b, target_a, target_b, own_ref, up_ref, down_ref):
-    kern = ids_ref[1]
-    odd = lax.rem(kern, 2) == 1
+    pack_ref[...] = jnp.broadcast_to(jnp.concatenate(rows, axis=0)[None], pack_ref.shape)
 
     def cut(left, right, even_start, odd_start):
         left = jnp.where(kern > 0, left, 0.0)
@@ -75,42 +70,62 @@
     down_ref[32:48, :] = target[48:64]
 
 
-def window(ids, mask, target):
+def prepare(kern, assign, kernels, source_weight, mask, target):
     last = mask.shape[1] // 128 - 1
 
-    def left(step, ids):
-        return (0, jnp.maximum(lax.div(ids[1] + 1, 2) - 1, 0))
-
-    def right(step, ids):
-        return (0, jnp.minimum(lax.div(ids[1] + 1, 2), last))
-
+    def left(step, kern):
+        return (0, jnp.maximum(lax.div(kern[0] + 1, 2) - 1, 0))
+
+    def right(step, kern):
+        return (0, jnp.minimum(lax.div(kern[0] + 1, 2), last))
+
+    def zeros(rank):
+        return lambda step, kern: (0,) * rank
+
+    mask, target = in_hbm(mask), in_hbm(target)
     return pl.pallas_call(
-        window_kernel,
+        prepare_kernel,
         grid_spec=pltpu.PrefetchScalarGridSpec(
             num_scalar_prefetch=1,
             grid=(1,),
             in_specs=[
+                pl.BlockSpec((1, 1), zeros(2)),
+                pl.BlockSpec((SPAN, 2, SPAN), zeros(3)),
+                pl.BlockSpec((1, SOURCES), zeros(2)),
                 pl.BlockSpec((OWN, 128), left),
                 pl.BlockSpec((OWN, 128), right),
                 pl.BlockSpec((OWN, 128), left),
                 pl.BlockSpec((OWN, 128), right),
             ],
             out_specs=[
-                pl.BlockSpec((128, 128), lambda step, ids: (0, 0)),
-                pl.BlockSpec((48, 128), lambda step, ids: (0, 0)),
-                pl.BlockSpec((48, 128), lambda step, ids: (0, 0)),
+                pl.BlockSpec((SOURCES, 8, 128), zeros(3)),
+                pl.BlockSpec((128, 128), zeros(2)),
+                pl.BlockSpec((48, 128), zeros(2)),
+                pl.BlockSpec((48, 128), zeros(2)),
             ],
+            scratch_shapes=[VMEM((48, 128), jnp.float32)],
         ),
         out_shape=[
+            jax.ShapeDtypeStruct((SOURCES, 8, 128), jnp.float32),
             jax.ShapeDtypeStruct((128, 128), jnp.bfloat16),
             jax.ShapeDtypeStruct((48, 128), jnp.bfloat16),
             jax.ShapeDtypeStruct((48, 128), jnp.bfloat16),
         ],
-        name="window",
-    )(ids, mask, mask, target, target)
-
-
-def columns_kernel(ids_ref, own_ref, before_ref, after_ref, cols_ref, aux_ref, side, rows):
+        compiler_params=pltpu.CompilerParams(vmem_limit_bytes=8 << 20),
+        name="prepare",
+    )(
+        kern,
+        assign.reshape(1, 1),
+        in_hbm(kernels.transpose(0, 2, 1, 3).reshape(SPAN, 2, SPAN)),
+        in_hbm(source_weight.reshape(1, SOURCES)),
+        mask,
+        mask,
+        target,
+        target,
+    )
+
+
+def columns_kernel(tile_ref, kern_ref, own_ref, before_ref, after_ref, cols_ref, aux_ref, side, rows):
     f32 = jnp.float32
     side[0:48, :] = before_ref[...].astype(f32)
     side[48:96, :] = after_ref[...].astype(f32)
@@ -122,9 +137,9 @@
     aux_ref[0, 10:74, :] = own_ref[64:128, :].astype(f32)
     aux_ref[0, 74:84, :] = side[80:90, :]
     aux_ref[0, 84:88, :] = jnp.zeros((4, 128), f32)
-    row = lax.broadcasted_iota(jnp.int32, (88, 128), 0) + (OWN * ids_ref[0] - HALF)
-    col = lax.broadcasted_iota(jnp.int32, (88, 128), 1) + (OWN * ids_ref[1] - HALF)
-    inside = (row >= 0) & (row < ids_ref[2]) & (col >= 0) & (col < ids_ref[3])
+    row = lax.broadcasted_iota(jnp.int32, (88, 128), 0) + (OWN * tile_ref[0] - HALF)
+    col = lax.broadcasted_iota(jnp.int32, (88, 128), 1) + (OWN * kern_ref[0] - HALF)
+    inside = (row >= 0) & (row < OWN * TILES) & (col >= 0) & (col < OWN * SOURCES)
     aux_ref[1, :, :] = jnp.where(inside, 2.0 * SLOPE, 0.0)
     base = [rows[0:104, :], rows[4:108, :]]
     for first in range(0, SPAN, 2):
@@ -145,29 +160,30 @@
             cols_ref[DEPTH * first : DEPTH * first + block.shape[0], 128 * group : 128 * group + 128] = block
 
 
-def columns(ids, own, before, after):
+def columns(tile, kern, own, before, after):
     return pl.pallas_call(
         columns_kernel,
         out_shape=[
             jax.ShapeDtypeStruct((TAPS, 256 * CHUNKS), jnp.bfloat16),
             jax.ShapeDtypeStruct((2, 88, 128), jnp.float32),
         ],
-        in_specs=[pl.BlockSpec(memory_space=pltpu.SMEM)] + [pl.BlockSpec(memory_space=VMEM)] * 3,
+        in_specs=[pl.BlockSpec(memory_space=pltpu.SMEM)] * 2 + [pl.BlockSpec(memory_space=VMEM)] * 3,
         out_specs=[pl.BlockSpec(memory_space=VMEM)] * 2,
         scratch_shapes=[VMEM((96, 128), jnp.float32), VMEM((112, 128), jnp.float32)],
+        compiler_params=pltpu.CompilerParams(vmem_limit_bytes=12 << 20),
+        cost_estimate=pl.CostEstimate(flops=1 << 20, bytes_accessed=4 << 20, transcendentals=0),
         name="columns",
-    )(ids, own, before, after)
-
-
-def image_kernel(weight_ref, taps_ref, cols_ref, aux_ref, grad_ref, resist_ref, matrix, sums, seen, final):
+    )(tile, kern, own, before, after)
+
+
+def image_kernel(taps_ref, cols_ref, aux_ref, grad_ref, resist_ref, matrix, sums, seen, final):
     f32 = jnp.float32
     base = jnp.concatenate([taps_ref[pl.ds(q, CHANNELS, stride=4), :] for q in range(4)], axis=1)
     weight = base[:, WEIGHT_SLOT : WEIGHT_SLOT + 1]
     for p in range(4):
         moved = pltpu.roll(base, p, 1) if p else base
         matrix[CHANNELS * p : CHANNELS * (p + 1), :] = moved.astype(jnp.bfloat16)
-    total = jnp.sum(weight_ref[...], axis=1, keepdims=True)
-    inverse = 1.0 / total
+    inverse = 1.0 / base[0:1, TOTAL_SLOT : TOTAL_SLOT + 1]
     factor = 2.0 * weight * inverse
     for n in range(CHUNKS):
         fields = jnp.dot(matrix[...], cols_ref[:, 256 * n : 256 * n + 256], preferred_element_type=f32)
@@ -209,7 +225,7 @@
     resist_ref[...] = pltpu.roll(seen[10:74, :], 118, 1)[:, :OWN]
 
 
-def image(source_weight, taps, cols, aux):
+def image(taps, cols, aux):
     flops = 2 * 2 * 4 * CHANNELS * TAPS * 256 * CHUNKS
     return pl.pallas_call(
         image_kernel,
@@ -217,7 +233,7 @@
             jax.ShapeDtypeStruct((OWN, OWN), jnp.float32),
             jax.ShapeDtypeStruct((OWN, OWN), jnp.float32),
         ],
-        in_specs=[pl.BlockSpec(memory_space=VMEM)] * 4,
+        in_specs=[pl.BlockSpec(memory_space=VMEM)] * 3,
         out_specs=[pl.BlockSpec(memory_space=VMEM)] * 2,
         scratch_shapes=[
             VMEM((4 * CHANNELS, TAPS), jnp.bfloat16),
@@ -226,20 +242,21 @@
             VMEM((72, 128), jnp.float32),
         ],
         cost_estimate=pl.CostEstimate(flops=flops, bytes_accessed=4 << 20, transcendentals=0),
+        compiler_params=pltpu.CompilerParams(vmem_limit_bytes=20 << 20),
         name="image",
-    )(source_weight.reshape(1, SOURCES), taps, cols, aux)
+    )(taps, cols, aux)
 
 
 def on_device(mask, target, kernels, source_weight, assign):
     tiles = lax.axis_size("tile")
-    tile, kern = lax.axis_index("tile"), lax.axis_index("kern")
-    ids = jnp.stack([tile, kern, tiles * mask.shape[0], mask.shape[1]]).astype(jnp.int32)
-    taps = lax.all_to_all(pack(assign, kernels, source_weight), "kern", split_axis=0, concat_axis=0, tiled=True)
-    own, up, down = window(ids, mask, target)
+    tile = lax.axis_index("tile").astype(jnp.int32).reshape(1)
+    kern = lax.axis_index("kern").astype(jnp.int32).reshape(1)
+    sent, own, up, down = prepare(kern, assign, kernels, source_weight, mask, target)
+    taps = lax.all_to_all(sent, "kern", split_axis=0, concat_axis=0, tiled=True)
     before = lax.ppermute(down, "tile", [(i, i + 1) for i in range(tiles - 1)])
     after = lax.ppermute(up, "tile", [(i + 1, i) for i in range(tiles - 1)])
-    cols, aux = columns(ids, own, before, after)
-    grad, resist = image(source_weight, taps.reshape(SOURCES * 8, 128), cols, aux)
+    cols, aux = columns(tile, kern, own, before, after)
+    grad, resist = image(taps.reshape(SOURCES * 8, 128), cols, aux)
     return (grad, resist)
 
 

time: 43.3 us -> 34.9 us (0.81)
  the two profiles are of different devices: /device:TPU:15 before, /device:TPU:2 now
where the time goes in v2:
time: 34.9 us; the launch traced here: 34.6 us
  starting transfers between devices  21.5 us (62%)
  waiting for transfers between devices  6.71 us (19%)
  Pallas kernels  5.05 us (14%)
  between operations  1.32 us (4%)
    all_to_all x1, starting transfers between devices, on_device(): taps = lax.all_to_all(sent, 'kern', split_axis=0, concat_axis=0, tiled=True)  16 us
    all_to_all x1, waiting for transfers between devices, on_device(): taps = lax.all_to_all(sent, 'kern', split_axis=0, concat_axis=0, tiled=True)  5.34 us
    ppermute x1, starting transfers between devices, on_device(): after = lax.ppermute(up, 'tile', [(i + 1, i) for i in range(tiles - 1)])  3.64 us
    pallas_call x1, Pallas kernels, image(): pl.pallas_call(image_kernel, out_shape=[jax.ShapeDtypeStruct((OWN, OWN),...  2.9 us
    ppermute x1, starting transfers between devices, on_device(): before = lax.ppermute(down, 'tile', [(i, i + 1) for i in range(tiles - 1)])  1.92 us
    pallas_call x1, Pallas kernels, prepare(): pl.pallas_call(prepare_kernel, grid_spec=pltpu.PrefetchScalarGridSpec(num...  1.7 us
    ppermute x1, waiting for transfers between devices, on_device(): after = lax.ppermute(up, 'tile', [(i + 1, i) for i in range(tiles - 1)])  1.37 us
  transfers between devices with their start and end apart: 3, of which 2 were waited for; matrix products, arithmetic and copies ran while one was open for 0% of the time, Pallas kernels for 1%

profile of v2, /device:TPU:2, one launch (start us, length us, event | category | flops | bytes accessed | tf_op | source)
XLA Modules:
  0.0 34.6 jit_solution(15396492413323401994)
XLA Ops:
  1.3 1.7 %prepare.1 = (f32[32,8,128]{2,1,0:T(8,128)}, bf16[128,128]{1,0:T(8,128)(2,1)S(1)}, bf16[48,128]{1,0:T(8,128)(2,1)S(1)}, bf16[48,128]{1,0:T(8,128)(2,1)S(1)}) custom-call(s32[1]{0:T(128)} %bitcast.kern_ref, s32[1,1]{1,0:T(1,128)} %bitcast.8.assign_ref, bf16[21,2,21]{2,1,0:T(2,128)(2,1)} %bitcast.10, f32[1,32]{1,0:T(1,128)} %bitcast.11, f32[64,2048]{1,0:T(8,128)} %mask_b.1, ...), custom_call_target="tpu_custom_call" | custom-call | tf_op jit(solution)/shard_map/prepare/pallas_call | solution.py:86
  3.0 16.0 %all-to-all-start = ((f32[32,8,128]{2,1,0:T(8,128)}), f32[32,8,128]{2,1,0:T(8,128)S(1)}, u32[]{:S(2)}, u32[]{:S(2)}) async-start(f32[32,8,128]{2,1,0:T(8,128)} %get-tuple-element.8), calls=%async_computation | async-start | bytes 262144 | tf_op jit(solution)/shard_map/all_to_all | solution.py:255
  18.9 1.9 %collective-permute-start = (bf16[48,128]{1,0:T(8,128)(2,1)S(1)}, bf16[48,128]{1,0:T(8,128)(2,1)S(1)}, u32[]{:S(2)}, u32[]{:S(2)}) collective-permute-start(bf16[48,128]{1,0:T(8,128)(2,1)S(1)} %get-tuple-element.10), channel_id=1, source_target_pairs={{0,32},{32,64},{64,96},{96,128},{128,160},{160,192},{192,224},{224... | collective-permute-start | bytes 36872 | tf_op jit(solution)/shard_map/ppermute | solution.py:256
  20.9 3.6 %collective-permute-start.1 = (bf16[48,128]{1,0:T(8,128)(2,1)S(1)}, bf16[48,128]{1,0:T(8,128)(2,1)S(1)}, u32[]{:S(2)}, u32[]{:S(2)}) collective-permute-start(bf16[48,128]{1,0:T(8,128)(2,1)S(1)} %get-tuple-element.11), channel_id=1, source_target_pairs={{32,0},{64,32},{96,64},{128,96},{160,128},{192,160},{224,192},{256... | collective-permute-start | bytes 36872 | tf_op jit(solution)/shard_map/ppermute | solution.py:257
  24.5 0.0 collective-permute-done.before_ref
  24.5 1.4 %collective-permute-done.1.after_ref = bf16[48,128]{1,0:T(8,128)(2,1)S(1)} collective-permute-done((bf16[48,128]{1,0:T(8,128)(2,1)S(1)}, bf16[48,128]{1,0:T(8,128)(2,1)S(1)}, u32[]{:S(2)}, u32[]{:S(2)}) %collective-permute-start.1) | collective-permute-done | bytes 12320 | tf_op jit(solution)/shard_map/ppermute | solution.py:257
  25.9 0.4 %columns.1 = (bf16[512,2816]{1,0:T(8,128)(2,1)S(1)}, f32[2,88,128]{2,1,0:T(8,128)S(1)}) custom-call(s32[1]{0:T(128)} %bitcast.6.tile_ref, s32[1]{0:T(128)} %bitcast.kern_ref, bf16[128,128]{1,0:T(8,128)(2,1)S(1)} %get-tuple-element.9.own_ref, bf16[48,128]{1,0:T(8,128)(2,1)S(1)} %collective-permute-done.before_ref, ...), custom_call_target="tpu_custom_call" | custom-call | flops 1048576 | bytes 4194304 | tf_op jit(solution)/shard_map/columns/pallas_call | solution.py:164
  26.4 5.3 %all-to-all-done = f32[32,8,128]{2,1,0:T(8,128)S(1)} async-done(((f32[32,8,128]{2,1,0:T(8,128)}), f32[32,8,128]{2,1,0:T(8,128)S(1)}, u32[]{:S(2)}, u32[]{:S(2)}) %all-to-all-start) | async-done | bytes 131104 | tf_op jit(solution)/shard_map/all_to_all | solution.py:255
  31.7 2.9 %image.1 = (f32[64,64]{1,0:T(8,128)}, f32[64,64]{1,0:T(8,128)}) custom-call(f32[256,128]{1,0:T(8,128)S(1)} %bitcast.9, bf16[512,2816]{1,0:T(8,128)(2,1)S(1)} %get-tuple-element.12.cols_ref, f32[2,88,128]{2,1,0:T(8,128)S(1)} %get-tuple-element.13.aux_ref), custom_call_target="tpu_custom_call" | custom-call | flops 1476395008 | bytes 4194304 | tf_op jit(solution)/shard_map/image/pallas_call | solution.py:230
Async XLA Ops:
  3.0 28.7 %all-to-all-start = ((f32[32,8,128]{2,1,0:T(8,128)}), f32[32,8,128]{2,1,0:T(8,128)S(1)}, u32[]{:S(2)}, u32[]{:S(2)}) async-start(f32[32,8,128]{2,1,0:T(8,128)} %get-tuple-element.8), calls=%async_computation | async-start | bytes 262144 | tf_op jit(solution)/shard_map/all_to_all | solution.py:255
  18.9 5.6 %collective-permute-start = (bf16[48,128]{1,0:T(8,128)(2,1)S(1)}, bf16[48,128]{1,0:T(8,128)(2,1)S(1)}, u32[]{:S(2)}, u32[]{:S(2)}) collective-permute-start(bf16[48,128]{1,0:T(8,128)(2,1)S(1)} %get-tuple-element.10), channel_id=1, source_target_pairs={{0,32},{32,64},{64,96},{96,128},{128,160},{160,192},{192,224},{224... | collective-permute-start | bytes 36872 | tf_op jit(solution)/shard_map/ppermute | solution.py:256
  20.9 5.0 %collective-permute-start.1 = (bf16[48,128]{1,0:T(8,128)(2,1)S(1)}, bf16[48,128]{1,0:T(8,128)(2,1)S(1)}, u32[]{:S(2)}, u32[]{:S(2)}) collective-permute-start(bf16[48,128]{1,0:T(8,128)(2,1)S(1)} %get-tuple-element.11), channel_id=1, source_target_pairs={{32,0},{64,32},{96,64},{128,96},{160,128},{192,160},{224,192},{256... | collective-permute-start | bytes 36872 | tf_op jit(solution)/shard_map/ppermute | solution.py:257

commit v3 on v2

v3 whole, which is shorter than its diff:
```python
import jax
import jax.numpy as jnp
from jax import lax
from jax.experimental import pallas as pl
from jax.experimental.pallas import tpu as pltpu
from jax.sharding import PartitionSpec as P

OWN = 64
SPAN = 21
HALF = 10
SOURCES = 32
CHANNELS = 2 * SOURCES
TILES = 16
DEPTH = 24
TAPS = 512
WEIGHT_SLOT = SPAN * DEPTH
CHUNKS = 11
BAND = 8 * SPAN + 8
SLOPE = 4.0
LEVEL = 0.6
VMEM = pltpu.VMEM


def in_hbm(array):
    return pltpu.with_memory_space_constraint(array, pltpu.HBM)


def pack_kernel(assign_ref, taps_ref, weight_ref, pack_ref, flat_ref):
    flat_ref[...] = jnp.zeros_like(flat_ref)
    for i in range(SPAN):
        flat_ref[2 * i : 2 * i + 2, 0:SPAN] = taps_ref[i].astype(jnp.float32)
    slot = lax.broadcasted_iota(jnp.int32, (128, TAPS), 1)
    low = DEPTH * lax.broadcasted_iota(jnp.int32, (128, TAPS), 0)
    spread = ((slot >= low) & (slot < low + DEPTH)).astype(jnp.float32).astype(jnp.bfloat16)
    wide = jnp.dot(flat_ref[...].astype(jnp.bfloat16), spread, preferred_element_type=jnp.float32)
    place = lax.broadcasted_iota(jnp.int32, wide.shape, 1).astype(jnp.float32)
    inner = place - DEPTH * jnp.floor((place + 0.5) * (1.0 / DEPTH))
    twice = 2.0 * inner
    row = lax.broadcasted_iota(jnp.int32, wide.shape, 0).astype(jnp.float32)
    index = lax.broadcasted_iota(jnp.int32, (1, SOURCES), 1)
    weight = jnp.sum(jnp.where(index == assign_ref[...], weight_ref[...], 0.0), axis=1, keepdims=True)
    lane = lax.broadcasted_iota(jnp.int32, (1, TAPS), 1)
    first = weight.astype(jnp.bfloat16).astype(jnp.float32)
    second = (weight - first).astype(jnp.bfloat16).astype(jnp.float32)
    third = weight - first - second
    rows = []
    for part in range(2):
        flat = jnp.sum(jnp.where(row == twice + part, wide, 0.0), axis=0, keepdims=True)
        for place, value in enumerate((first, second, third)):
            flat = jnp.where(lane == WEIGHT_SLOT + place, value, flat)
        rows += [flat[:, 128 * q : 128 * q + 128] for q in range(4)]
    pack_ref[...] = jnp.broadcast_to(jnp.concatenate(rows, axis=0).astype(jnp.bfloat16)[None], pack_ref.shape)


def pack(assign, kernels, source_weight):
    return pl.pallas_call(
        pack_kernel,
        out_shape=jax.ShapeDtypeStruct((SOURCES, 8, 128), jnp.bfloat16),
        in_specs=[pl.BlockSpec(memory_space=VMEM)] * 3,
        out_specs=pl.BlockSpec(memory_space=VMEM),
        scratch_shapes=[VMEM((48, 128), jnp.float32)],
        compiler_params=pltpu.CompilerParams(vmem_limit_bytes=8 << 20),
        name="pack",
    )(
        assign.reshape(1, 1),
        in_hbm(kernels.transpose(0, 2, 1, 3).reshape(SPAN, 2, SPAN)),
        in_hbm(source_weight.reshape(1, SOURCES)),
    )


def window_kernel(tile_ref, kern_ref, mask_a, mask_b, target_a, target_b, own_ref, near_ref, far_ref):
    kern = kern_ref[0]
    odd = lax.rem(kern, 2) == 1

    def cut(left, right, even_start, odd_start):
        left = jnp.where(kern > 0, left, 0.0)
        right = jnp.where(kern < SOURCES - 1, right, 0.0)
        both = jnp.concatenate([left, right], axis=1)
        even = pltpu.roll(both, 256 - even_start, 1)[:, :128]
        other = pltpu.roll(both, 256 - odd_start, 1)[:, :128]
        return jnp.where(odd, other, even).astype(jnp.bfloat16)

    mask = cut(mask_a[...], mask_b[...], 108, 44)
    target = cut(target_a[...].astype(jnp.float32), target_b[...].astype(jnp.float32), 118, 54)
    own_ref[0:64, :] = mask
    own_ref[64:128, :] = target
    even = lax.rem(tile_ref[0], 2) == 0
    near_ref[0:32, :] = jnp.where(even, mask[32:64], mask[0:32])
    near_ref[32:48, :] = jnp.where(even, target[48:64], target[0:16])
    far_ref[0:32, :] = jnp.where(even, mask[0:32], mask[32:64])
    far_ref[32:48, :] = jnp.where(even, target[0:16], target[48:64])


def window(tile, kern, mask, target):
    last = mask.shape[1] // 128 - 1

    def left(step, tile, kern):
        return (0, jnp.maximum(lax.div(kern[0] + 1, 2) - 1, 0))

    def right(step, tile, kern):
        return (0, jnp.minimum(lax.div(kern[0] + 1, 2), last))

    def zeros(rank):
        return lambda step, tile, kern: (0,) * rank

    mask, target = in_hbm(mask), in_hbm(target)
    return pl.pallas_call(
        window_kernel,
        grid_spec=pltpu.PrefetchScalarGridSpec(
            num_scalar_prefetch=2,
            grid=(1,),
            in_specs=[
                pl.BlockSpec((OWN, 128), left),
                pl.BlockSpec((OWN, 128), right),
                pl.BlockSpec((OWN, 128), left),
                pl.BlockSpec((OWN, 128), right),
            ],
            out_specs=[
                pl.BlockSpec((128, 128), zeros(2)),
                pl.BlockSpec((48, 128), zeros(2)),
                pl.BlockSpec((48, 128), zeros(2)),
            ],
        ),
        out_shape=[
            jax.ShapeDtypeStruct((128, 128), jnp.bfloat16),
            jax.ShapeDtypeStruct((48, 128), jnp.bfloat16),
            jax.ShapeDtypeStruct((48, 128), jnp.bfloat16),
        ],
        compiler_params=pltpu.CompilerParams(vmem_limit_bytes=8 << 20),
        name="window",
    )(
        tile,
        kern,
        mask,
        mask,
        target,
        target,
    )


def columns_kernel(tile_ref, kern_ref, own_ref, near_ref, far_ref, cols_ref, aux_ref, side, rows):
    f32 = jnp.float32
    even = lax.rem(tile_ref[0], 2) == 0
    near, far = near_ref[...].astype(f32), far_ref[...].astype(f32)
    side[0:48, :] = jnp.where(even, far, near)
    side[48:96, :] = jnp.where(even, near, far)
    rows[0:20, :] = side[12:32, :]
    rows[20:84, :] = own_ref[0:64, :].astype(f32)
    rows[84:104, :] = side[48:68, :]
    rows[104:112, :] = jnp.zeros((8, 128), f32)
    aux_ref[0, 0:10, :] = side[38:48, :]
    aux_ref[0, 10:74, :] = own_ref[64:128, :].astype(f32)
    aux_ref[0, 74:84, :] = side[80:90, :]
    aux_ref[0, 84:88, :] = jnp.zeros((4, 128), f32)
    row = lax.broadcasted_iota(jnp.int32, (88, 128), 0) + (OWN * tile_ref[0] - HALF)
    col = lax.broadcasted_iota(jnp.int32, (88, 128), 1) + (OWN * kern_ref[0] - HALF)
    inside = (row >= 0) & (row < OWN * TILES) & (col >= 0) & (col < OWN * SOURCES)
    aux_ref[1, :, :] = jnp.where(inside, 2.0 * SLOPE, 0.0)
    base = [rows[0:104, :], rows[4:108, :]]
    for first in range(0, SPAN, 2):
        turned = []
        for tap in (first, first + 1):
            if tap >= SPAN:
                turned.append(None)
            else:
                turned.append([pltpu.roll(b, 128 - tap, 1) if tap else b for b in base])
        for group in range(2 * CHUNKS):
            at = 8 * (group // 2)
            one = turned[0][group % 2][at : at + 24]
            if turned[1] is None:
                two = jnp.zeros((8, 128), f32)
            else:
                two = turned[1][group % 2][at : at + 24]
            block = jnp.concatenate([one, two], axis=0).astype(jnp.bfloat16)
            cols_ref[DEPTH * first : DEPTH * first + block.shape[0], 128 * group : 128 * group + 128] = block


def columns(tile, kern, own, near, far):
    return pl.pallas_call(
        columns_kernel,
        out_shape=[
            jax.ShapeDtypeStruct((TAPS, 256 * CHUNKS), jnp.bfloat16),
            jax.ShapeDtypeStruct((2, 88, 128), jnp.float32),
        ],
        in_specs=[pl.BlockSpec(memory_space=pltpu.SMEM)] * 2 + [pl.BlockSpec(memory_space=VMEM)] * 3,
        out_specs=[pl.BlockSpec(memory_space=VMEM)] * 2,
        scratch_shapes=[VMEM((96, 128), jnp.float32), VMEM((112, 128), jnp.float32)],
        compiler_params=pltpu.CompilerParams(vmem_limit_bytes=12 << 20),
        cost_estimate=pl.CostEstimate(flops=1 << 20, bytes_accessed=4 << 20, transcendentals=0),
        name="columns",
    )(tile, kern, own, near, far)


def image_kernel(taps_ref, cols_ref, aux_ref, grad_ref, resist_ref, wide, matrix, turned, fields, adjoint, sums, seen, final):
    f32 = jnp.float32
    wide[...] = taps_ref[...].astype(f32)
    base = jnp.concatenate([wide[pl.ds(q, CHANNELS, stride=4), :] for q in range(4)], axis=1)
    weight = base[:, WEIGHT_SLOT : WEIGHT_SLOT + 1] + base[:, WEIGHT_SLOT + 1 : WEIGHT_SLOT + 2]
    weight = weight + base[:, WEIGHT_SLOT + 2 : WEIGHT_SLOT + 3]
    moved = jnp.concatenate([pltpu.roll(base, p, 1) if p else base for p in range(4)], axis=0)
    matrix[...] = moved.astype(jnp.bfloat16)
    upright = jnp.transpose(moved)
    for third in range(3):
        starts = [DEPTH * tap + 8 * third for tap in range(SPAN)]
        rows = [upright[at : at + 8] for at in starts] + [jnp.zeros((8, 4 * CHANNELS), f32)]
        turned[BAND * third : BAND * (third + 1), :] = jnp.concatenate(rows, axis=0).astype(jnp.bfloat16)
    inverse = 2.0 / jnp.sum(weight, axis=0, keepdims=True)
    twice = 2.0 * inverse
    def groups_of(n):
        return [2 * n, 2 * n + 1] if n < CHUNKS - 1 else [2 * n]

    def image_of(n):
        width = 128 * len(groups_of(n))
        cols = cols_ref[:, 256 * n : 256 * n + width]
        fields[n % 2, :, 0:width] = jnp.dot(matrix[...], cols, preferred_element_type=f32)

    def adjoint_of(n):
        groups = groups_of(n)
        width = 128 * len(groups)
        for p in range(4):
            field = fields[n % 2, CHANNELS * p : CHANNELS * (p + 1), 0:width]
            heavy = weight * field
            aerial = jnp.sum(heavy * field, axis=0, keepdims=True) * inverse
            resist = jax.nn.sigmoid(SLOPE * (aerial - LEVEL))
            spots = [4 * group + p for group in groups]
            target = jnp.concatenate([aux_ref[0, spot : spot + 1, :] for spot in spots], axis=1)
            scale = jnp.concatenate([aux_ref[1, spot : spot + 1, :] for spot in spots], axis=1)
            sense = scale * (resist - target) * resist * (1.0 - resist)
            for parity, spot in enumerate(spots):
                seen[spot : spot + 1, :] = resist[:, 128 * parity : 128 * parity + 128]
            value = (heavy * (twice * sense)).astype(jnp.bfloat16)
            adjoint[n % 2, CHANNELS * p : CHANNELS * (p + 1), 0:width] = value

    def spread_of(n):
        groups = groups_of(n)
        low, high = max(0, 2 - n), min(3, 11 - n)
        moved_in = adjoint[n % 2, :, 0 : 128 * len(groups)]
        spread = jnp.dot(turned[BAND * low : BAND * high, :], moved_in, preferred_element_type=f32)
        for third in range(low, high):
            tile = n + third
            for parity in range(len(groups)):
                if tile > 10 - parity:
                    continue
                at = BAND * (third - low)
                piece = spread[at : at + 8 * SPAN, 128 * parity : 128 * parity + 128]
                if third == 2:
                    sums[parity, tile - 2, :, :] = piece
                else:
                    sums[parity, tile - 2, :, :] += piece

    for step in range(CHUNKS + 2):
        if step < CHUNKS:
            image_of(step)
        if 0 <= step - 2:
            spread_of(step - 2)
        if 0 <= step - 1 < CHUNKS:
            adjoint_of(step - 1)
    totals = []
    for parity in range(2):
        total = None
        for tap in range(SPAN):
            part = jnp.concatenate([sums[parity, at, 8 * tap : 8 * tap + 8, :] for at in range(9 - parity)], axis=0)
            part = pltpu.roll(part, tap, 1) if tap else part
            total = part if total is None else total + part
        totals.append(total)
    final[...] = totals[0]
    grad = final[4:68, :] + totals[1]
    grad_ref[...] = pltpu.roll(grad, 108, 1)[:, :OWN]
    resist_ref[...] = pltpu.roll(seen[10:74, :], 118, 1)[:, :OWN]


def image(taps, cols, aux):
    flops = 2 * 2 * 4 * CHANNELS * TAPS * 256 * CHUNKS
    return pl.pallas_call(
        image_kernel,
        out_shape=[
            jax.ShapeDtypeStruct((OWN, OWN), jnp.float32),
            jax.ShapeDtypeStruct((OWN, OWN), jnp.float32),
        ],
        in_specs=[pl.BlockSpec(memory_space=VMEM)] * 3,
        out_specs=[pl.BlockSpec(memory_space=VMEM)] * 2,
        scratch_shapes=[
            VMEM((8 * SOURCES, 128), jnp.float32),
            VMEM((4 * CHANNELS, TAPS), jnp.bfloat16),
            VMEM((3 * BAND, 4 * CHANNELS), jnp.bfloat16),
            VMEM((2, 4 * CHANNELS, 256), jnp.float32),
            VMEM((2, 4 * CHANNELS, 256), jnp.bfloat16),
            VMEM((2, 9, 8 * SPAN, 128), jnp.float32),
            VMEM((88, 128), jnp.float32),
            VMEM((72, 128), jnp.float32),
        ],
        cost_estimate=pl.CostEstimate(flops=flops, bytes_accessed=4 << 20, transcendentals=0),
        compiler_params=pltpu.CompilerParams(vmem_limit_bytes=20 << 20),
        name="image",
    )(taps, cols, aux)


def on_device(mask, target, kernels, source_weight, assign):
    tiles = lax.axis_size("tile")
    tile = lax.axis_index("tile").astype(jnp.int32).reshape(1)
    kern = lax.axis_index("kern").astype(jnp.int32).reshape(1)
    sent = pack(assign, kernels, source_weight)
    own, near, far = window(tile, kern, mask, target)
    taps = lax.all_to_all(sent, "kern", split_axis=0, concat_axis=0, tiled=True)

    def swapped(part, first):
        pairs = [(i, i + 1) for i in range(first, tiles - 1, 2)]
        return lax.ppermute(part, "tile", pairs + [(j, i) for i, j in pairs])

    far = swapped(far, 1)
    near = swapped(near, 0)
    cols, aux = columns(tile, kern, own, near, far)
    grad, resist = image(taps.reshape(SOURCES * 8, 128), cols, aux)
    return (grad, resist)


def solution(mesh):
    placed = (P("tile", None), P("tile", None), P("kern", None, None, None), P(), P("kern"))
    return jax.shard_map(
        on_device,
        mesh=mesh,
        in_specs=placed,
        out_specs=(P("tile", "kern"), P("tile", "kern")),
        check_vma=False,
    )
```

time: 34.9 us -> 34.1 us (0.977)
  starting transfers between devices: 21.5 us -> 20.4 us
  Pallas kernels: 5.05 us -> 5.5 us
    all_to_all x1, waiting for transfers between devices: 5.34 us -> 4.07 us  [on_device(): taps = lax.all_to_all(sent, 'kern', split_axis=0, concat_axis=0, tiled=True)]
    ppermute x2, starting transfers between devices: 5.56 us -> 4.47 us  [swapped(): return lax.ppermute(part, 'tile', pairs + [(j, i) for i, j in pairs])]
    ppermute x2, waiting for transfers between devices: 1.37 us -> 2.45 us  [swapped(): return lax.ppermute(part, 'tile', pairs + [(j, i) for i, j in pairs])]
    pallas_call x1 -> x2, Pallas kernels: 1.7 us -> 2.47 us  [the longest x1 1.52 us: pack(): pl.pallas_call(pack_kernel, out_shape=jax.ShapeDtypeStruct((SOURCES, 8, 1...]
  transfers between devices with their start and end apart: 3 -> 3, of which waited for: 2 -> 2; matrix products, arithmetic and copies ran while one was open for 0% -> 0% of each run, Pallas kernels for 1% -> 4%
where the time goes in v3:
time: 34.1 us; the launch traced here: 33.8 us
  starting transfers between devices  20.4 us (60%)
  waiting for transfers between devices  6.52 us (19%)
  Pallas kernels  5.5 us (16%)
  between operations  1.33 us (4%)
    all_to_all x1, starting transfers between devices, on_device(): taps = lax.all_to_all(sent, 'kern', split_axis=0, concat_axis=0, tiled=True)  16 us
    ppermute x2, starting transfers between devices, swapped(): return lax.ppermute(part, 'tile', pairs + [(j, i) for i, j in pairs])  4.47 us
    all_to_all x1, waiting for transfers between devices, on_device(): taps = lax.all_to_all(sent, 'kern', split_axis=0, concat_axis=0, tiled=True)  4.07 us
    pallas_call x1, Pallas kernels, image(): pl.pallas_call(image_kernel, out_shape=[jax.ShapeDtypeStruct((OWN, OWN),...  2.59 us
    ppermute x2, waiting for transfers between devices, swapped(): return lax.ppermute(part, 'tile', pairs + [(j, i) for i, j in pairs])  2.45 us
    pallas_call x1, Pallas kernels, pack(): pl.pallas_call(pack_kernel, out_shape=jax.ShapeDtypeStruct((SOURCES, 8, 1...  1.52 us
    pallas_call x1, Pallas kernels, window(): pl.pallas_call(window_kernel, grid_spec=pltpu.PrefetchScalarGridSpec(num_...  0.95 us
  transfers between devices with their start and end apart: 3, of which 2 were waited for; matrix products, arithmetic and copies ran while one was open for 0% of the time, Pallas kernels for 4%

profile of v3, /device:TPU:2, one launch (start us, length us, event | category | flops | bytes accessed | tf_op | source)
XLA Modules:
  0.0 33.8 jit_solution(6666064377550951045)
XLA Ops:
  1.3 1.5 %pack.1 = bf16[32,8,128]{2,1,0:T(8,128)(2,1)} custom-call(s32[1,1]{1,0:T(1,128)} %bitcast.8.assign_ref, bf16[21,2,21]{2,1,0:T(2,128)(2,1)} %bitcast.10, f32[1,32]{1,0:T(1,128)} %bitcast.11), custom_call_target="tpu_custom_call" | custom-call | tf_op jit(solution)/shard_map/pack/pallas_call | solution.py:56
  2.8 16.0 %all-to-all-start = ((bf16[32,8,128]{2,1,0:T(8,128)(2,1)}), bf16[32,8,128]{2,1,0:T(8,128)(2,1)S(1)}, u32[]{:S(2)}, u32[]{:S(2)}) async-start(bf16[32,8,128]{2,1,0:T(8,128)(2,1)} %pack.1), calls=%async_computation | async-start | bytes 131072 | tf_op jit(solution)/shard_map/all_to_all | solution.py:304
  18.8 1.0 %window.1 = (bf16[128,128]{1,0:T(8,128)(2,1)S(1)}, bf16[48,128]{1,0:T(8,128)(2,1)S(1)}, bf16[48,128]{1,0:T(8,128)(2,1)S(1)}) custom-call(s32[1]{0:T(128)} %bitcast.5.tile_ref, s32[1]{0:T(128)} %bitcast.6.kern_ref, f32[64,2048]{1,0:T(8,128)} %mask_b.1, f32[64,2048]{1,0:T(8,128)} %mask_b.1, s32[64,2048]{1,0:T(8,128)} %target_b.1, s32[64,2048]{1,0:T(8,128)} %target_b.1), custom_call_target="tpu_custom_call" | custom-call | tf_op jit(solution)/shard_map/window/pallas_call | solution.py:107
  19.7 1.9 %collective-permute-start = (bf16[48,128]{1,0:T(8,128)(2,1)S(1)}, bf16[48,128]{1,0:T(8,128)(2,1)S(1)}, u32[]{:S(2)}, u32[]{:S(2)}) collective-permute-start(bf16[48,128]{1,0:T(8,128)(2,1)S(1)} %get-tuple-element.8), channel_id=1, source_target_pairs={{0,32},{64,96},{128,160},{192,224},{256,288},{320,352},{384,416},{... | collective-permute-start | bytes 36872 | tf_op jit(solution)/shard_map/ppermute | solution.py:308
  21.7 2.5 %collective-permute-start.1 = (bf16[48,128]{1,0:T(8,128)(2,1)S(1)}, bf16[48,128]{1,0:T(8,128)(2,1)S(1)}, u32[]{:S(2)}, u32[]{:S(2)}) collective-permute-start(bf16[48,128]{1,0:T(8,128)(2,1)S(1)} %get-tuple-element.9), channel_id=1, source_target_pairs={{32,64},{96,128},{160,192},{224,256},{288,320},{352,384},{416,448}... | collective-permute-start | bytes 36872 | tf_op jit(solution)/shard_map/ppermute | solution.py:308
  24.2 0.0 collective-permute-done.near_ref
  24.2 2.5 %collective-permute-done.1.far_ref = bf16[48,128]{1,0:T(8,128)(2,1)S(1)} collective-permute-done((bf16[48,128]{1,0:T(8,128)(2,1)S(1)}, bf16[48,128]{1,0:T(8,128)(2,1)S(1)}, u32[]{:S(2)}, u32[]{:S(2)}) %collective-permute-start.1) | collective-permute-done | bytes 12320 | tf_op jit(solution)/shard_map/ppermute | solution.py:308
  26.7 0.4 %columns.1 = (bf16[512,2816]{1,0:T(8,128)(2,1)S(1)}, f32[2,88,128]{2,1,0:T(8,128)S(1)}) custom-call(s32[1]{0:T(128)} %bitcast.5.tile_ref, s32[1]{0:T(128)} %bitcast.6.kern_ref, bf16[128,128]{1,0:T(8,128)(2,1)S(1)} %get-tuple-element.7.own_ref, bf16[48,128]{1,0:T(8,128)(2,1)S(1)} %collective-permute-done.near_ref, ...), custom_call_target="tpu_custom_call" | custom-call | flops 1048576 | bytes 4194304 | tf_op jit(solution)/shard_map/columns/pallas_call | solution.py:179
  27.1 4.1 %all-to-all-done = bf16[32,8,128]{2,1,0:T(8,128)(2,1)S(1)} async-done(((bf16[32,8,128]{2,1,0:T(8,128)(2,1)}), bf16[32,8,128]{2,1,0:T(8,128)(2,1)S(1)}, u32[]{:S(2)}, u32[]{:S(2)}) %all-to-all-start) | async-done | bytes 65568 | tf_op jit(solution)/shard_map/all_to_all | solution.py:304
  31.2 2.6 %image.1 = (f32[64,64]{1,0:T(8,128)}, f32[64,64]{1,0:T(8,128)}) custom-call(bf16[256,128]{1,0:T(8,128)(2,1)S(1)} %bitcast.9, bf16[512,2816]{1,0:T(8,128)(2,1)S(1)} %get-tuple-element.10.cols_ref, f32[2,88,128]{2,1,0:T(8,128)S(1)} %get-tuple-element.11.aux_ref), custom_call_target="tpu_custom_call" | custom-call | flops 1476395008 | bytes 4194304 | tf_op jit(solution)/shard_map/image/pallas_call | solution.py:274
Async XLA Ops:
  2.8 28.4 %all-to-all-start = ((bf16[32,8,128]{2,1,0:T(8,128)(2,1)}), bf16[32,8,128]{2,1,0:T(8,128)(2,1)S(1)}, u32[]{:S(2)}, u32[]{:S(2)}) async-start(bf16[32,8,128]{2,1,0:T(8,128)(2,1)} %pack.1), calls=%async_computation | async-start | bytes 131072 | tf_op jit(solution)/shard_map/all_to_all | solution.py:304
  19.7 4.5 %collective-permute-start = (bf16[48,128]{1,0:T(8,128)(2,1)S(1)}, bf16[48,128]{1,0:T(8,128)(2,1)S(1)}, u32[]{:S(2)}, u32[]{:S(2)}) collective-permute-start(bf16[48,128]{1,0:T(8,128)(2,1)S(1)} %get-tuple-element.8), channel_id=1, source_target_pairs={{0,32},{64,96},{128,160},{192,224},{256,288},{320,352},{384,416},{... | collective-permute-start | bytes 36872 | tf_op jit(solution)/shard_map/ppermute | solution.py:308
  21.7 5.0 %collective-permute-start.1 = (bf16[48,128]{1,0:T(8,128)(2,1)S(1)}, bf16[48,128]{1,0:T(8,128)(2,1)S(1)}, u32[]{:S(2)}, u32[]{:S(2)}) collective-permute-start(bf16[48,128]{1,0:T(8,128)(2,1)S(1)} %get-tuple-element.9), channel_id=1, source_target_pairs={{32,64},{96,128},{160,192},{224,256},{288,320},{352,384},{416,448}... | collective-permute-start | bytes 36872 | tf_op jit(solution)/shard_map/ppermute | solution.py:308

commit v4 on v3

--- a/solution.py
+++ b/solution.py
@@ -191,7 +191,7 @@
     )(tile, kern, own, near, far)
 
 
-def image_kernel(taps_ref, cols_ref, aux_ref, grad_ref, resist_ref, wide, matrix, turned, fields, adjoint, sums, seen, final):
+def image_kernel(taps_ref, cols_ref, aux_ref, grad_out, resist_out, grad_ref, resist_ref, done, wide, matrix, turned, fields, adjoint, sums, seen, final):
     f32 = jnp.float32
     wide[...] = taps_ref[...].astype(f32)
     base = jnp.concatenate([wide[pl.ds(q, CHANNELS, stride=4), :] for q in range(4)], axis=1)
@@ -243,10 +243,17 @@
                     continue
                 at = BAND * (third - low)
                 piece = spread[at : at + 8 * SPAN, 128 * parity : 128 * parity + 128]
+                spot = tile - 2
                 if third == 2:
-                    sums[parity, tile - 2, :, :] = piece
+                    sums[parity, spot, :, :] = piece
+                elif third == 1:
+                    sums[parity, spot, :, :] += piece
                 else:
-                    sums[parity, tile - 2, :, :] += piece
+                    piece = piece + sums[parity, spot, :, :]
+                    total = piece[0:8]
+                    for tap in range(1, SPAN):
+                        total = total + pltpu.roll(piece[8 * tap : 8 * tap + 8], tap, 1)
+                    final[parity, 8 * spot : 8 * spot + 8, :] = total
 
     for step in range(CHUNKS + 2):
         if step < CHUNKS:
@@ -255,18 +262,16 @@
             spread_of(step - 2)
         if 0 <= step - 1 < CHUNKS:
             adjoint_of(step - 1)
-    totals = []
-    for parity in range(2):
-        total = None
-        for tap in range(SPAN):
-            part = jnp.concatenate([sums[parity, at, 8 * tap : 8 * tap + 8, :] for at in range(9 - parity)], axis=0)
-            part = pltpu.roll(part, tap, 1) if tap else part
-            total = part if total is None else total + part
-        totals.append(total)
-    final[...] = totals[0]
-    grad = final[4:68, :] + totals[1]
+        if step == CHUNKS:
+            resist_ref[...] = pltpu.roll(seen[10:74, :], 118, 1)[:, :OWN]
+            resist_copy = pltpu.make_async_copy(resist_ref, resist_out, done.at[0])
+            resist_copy.start()
+    grad = final[0, 4:68, :] + final[1, 0:64, :]
     grad_ref[...] = pltpu.roll(grad, 108, 1)[:, :OWN]
-    resist_ref[...] = pltpu.roll(seen[10:74, :], 118, 1)[:, :OWN]
+    grad_copy = pltpu.make_async_copy(grad_ref, grad_out, done.at[1])
+    grad_copy.start()
+    resist_copy.wait()
+    grad_copy.wait()
 
 
 def image(taps, cols, aux):
@@ -278,8 +283,11 @@
             jax.ShapeDtypeStruct((OWN, OWN), jnp.float32),
         ],
         in_specs=[pl.BlockSpec(memory_space=VMEM)] * 3,
-        out_specs=[pl.BlockSpec(memory_space=VMEM)] * 2,
+        out_specs=[pl.BlockSpec(memory_space=pl.ANY)] * 2,
         scratch_shapes=[
+            VMEM((OWN, OWN), jnp.float32),
+            VMEM((OWN, OWN), jnp.float32),
+            pltpu.SemaphoreType.DMA((2,)),
             VMEM((8 * SOURCES, 128), jnp.float32),
             VMEM((4 * CHANNELS, TAPS), jnp.bfloat16),
             VMEM((3 * BAND, 4 * CHANNELS), jnp.bfloat16),
@@ -287,7 +295,7 @@
             VMEM((2, 4 * CHANNELS, 256), jnp.bfloat16),
             VMEM((2, 9, 8 * SPAN, 128), jnp.float32),
             VMEM((88, 128), jnp.float32),
-            VMEM((72, 128), jnp.float32),
+            VMEM((2, 72, 128), jnp.float32),
         ],
         cost_estimate=pl.CostEstimate(flops=flops, bytes_accessed=4 << 20, transcendentals=0),
         compiler_params=pltpu.CompilerParams(vmem_limit_bytes=20 << 20),

time: 34.1 us -> 34.1 us (level)
  no operation moved by 1% of the time
where the time goes in v4:
time: 34.1 us; the launch traced here: 33.8 us
  starting transfers between devices  20.4 us (60%)
  waiting for transfers between devices  6.52 us (19%)
  Pallas kernels  5.51 us (16%)
  between operations  1.33 us (4%)
    all_to_all x1, starting transfers between devices, on_device(): taps = lax.all_to_all(sent, 'kern', split_axis=0, concat_axis=0, tiled=True)  16 us
    ppermute x2, starting transfers between devices, swapped(): return lax.ppermute(part, 'tile', pairs + [(j, i) for i, j in pairs])  4.47 us
    all_to_all x1, waiting for transfers between devices, on_device(): taps = lax.all_to_all(sent, 'kern', split_axis=0, concat_axis=0, tiled=True)  4.07 us
    pallas_call x1, Pallas kernels, image(): pl.pallas_call(image_kernel, out_shape=[jax.ShapeDtypeStruct((OWN, OWN),...  2.6 us
    ppermute x2, waiting for transfers between devices, swapped(): return lax.ppermute(part, 'tile', pairs + [(j, i) for i, j in pairs])  2.45 us
    pallas_call x1, Pallas kernels, pack(): pl.pallas_call(pack_kernel, out_shape=jax.ShapeDtypeStruct((SOURCES, 8, 1...  1.52 us
    pallas_call x1, Pallas kernels, window(): pl.pallas_call(window_kernel, grid_spec=pltpu.PrefetchScalarGridSpec(num_...  0.95 us
  transfers between devices with their start and end apart: 3, of which 2 were waited for; matrix products, arithmetic and copies ran while one was open for 0% of the time, Pallas kernels for 4%

profile of v4, /device:TPU:2, one launch (start us, length us, event | category | flops | bytes accessed | tf_op | source)
XLA Modules:
  0.0 33.8 jit_solution(11362678428530679054)
XLA Ops:
  1.3 1.5 %pack.1 = bf16[32,8,128]{2,1,0:T(8,128)(2,1)} custom-call(s32[1,1]{1,0:T(1,128)} %bitcast.8.assign_ref, bf16[21,2,21]{2,1,0:T(2,128)(2,1)} %bitcast.10, f32[1,32]{1,0:T(1,128)} %bitcast.11), custom_call_target="tpu_custom_call" | custom-call | tf_op jit(solution)/shard_map/pack/pallas_call | solution.py:56
  2.8 16.0 %all-to-all-start = ((bf16[32,8,128]{2,1,0:T(8,128)(2,1)}), bf16[32,8,128]{2,1,0:T(8,128)(2,1)S(1)}, u32[]{:S(2)}, u32[]{:S(2)}) async-start(bf16[32,8,128]{2,1,0:T(8,128)(2,1)} %pack.1), calls=%async_computation | async-start | bytes 131072 | tf_op jit(solution)/shard_map/all_to_all | solution.py:312
  18.8 1.0 %window.1 = (bf16[128,128]{1,0:T(8,128)(2,1)S(1)}, bf16[48,128]{1,0:T(8,128)(2,1)S(1)}, bf16[48,128]{1,0:T(8,128)(2,1)S(1)}) custom-call(s32[1]{0:T(128)} %bitcast.5.tile_ref, s32[1]{0:T(128)} %bitcast.6.kern_ref, f32[64,2048]{1,0:T(8,128)} %mask_b.1, f32[64,2048]{1,0:T(8,128)} %mask_b.1, s32[64,2048]{1,0:T(8,128)} %target_b.1, s32[64,2048]{1,0:T(8,128)} %target_b.1), custom_call_target="tpu_custom_call" | custom-call | tf_op jit(solution)/shard_map/window/pallas_call | solution.py:107
  19.7 1.9 %collective-permute-start = (bf16[48,128]{1,0:T(8,128)(2,1)S(1)}, bf16[48,128]{1,0:T(8,128)(2,1)S(1)}, u32[]{:S(2)}, u32[]{:S(2)}) collective-permute-start(bf16[48,128]{1,0:T(8,128)(2,1)S(1)} %get-tuple-element.8), channel_id=1, source_target_pairs={{0,32},{64,96},{128,160},{192,224},{256,288},{320,352},{384,416},{... | collective-permute-start | bytes 36872 | tf_op jit(solution)/shard_map/ppermute | solution.py:316
  21.7 2.5 %collective-permute-start.1 = (bf16[48,128]{1,0:T(8,128)(2,1)S(1)}, bf16[48,128]{1,0:T(8,128)(2,1)S(1)}, u32[]{:S(2)}, u32[]{:S(2)}) collective-permute-start(bf16[48,128]{1,0:T(8,128)(2,1)S(1)} %get-tuple-element.9), channel_id=1, source_target_pairs={{32,64},{96,128},{160,192},{224,256},{288,320},{352,384},{416,448}... | collective-permute-start | bytes 36872 | tf_op jit(solution)/shard_map/ppermute | solution.py:316
  24.2 0.0 collective-permute-done.near_ref
  24.2 2.5 %collective-permute-done.1.far_ref = bf16[48,128]{1,0:T(8,128)(2,1)S(1)} collective-permute-done((bf16[48,128]{1,0:T(8,128)(2,1)S(1)}, bf16[48,128]{1,0:T(8,128)(2,1)S(1)}, u32[]{:S(2)}, u32[]{:S(2)}) %collective-permute-start.1) | collective-permute-done | bytes 12320 | tf_op jit(solution)/shard_map/ppermute | solution.py:316
  26.7 0.4 %columns.1 = (bf16[512,2816]{1,0:T(8,128)(2,1)S(1)}, f32[2,88,128]{2,1,0:T(8,128)S(1)}) custom-call(s32[1]{0:T(128)} %bitcast.5.tile_ref, s32[1]{0:T(128)} %bitcast.6.kern_ref, bf16[128,128]{1,0:T(8,128)(2,1)S(1)} %get-tuple-element.7.own_ref, bf16[48,128]{1,0:T(8,128)(2,1)S(1)} %collective-permute-done.near_ref, ...), custom_call_target="tpu_custom_call" | custom-call | flops 1048576 | bytes 4194304 | tf_op jit(solution)/shard_map/columns/pallas_call | solution.py:179
  27.1 4.1 %all-to-all-done = bf16[32,8,128]{2,1,0:T(8,128)(2,1)S(1)} async-done(((bf16[32,8,128]{2,1,0:T(8,128)(2,1)}), bf16[32,8,128]{2,1,0:T(8,128)(2,1)S(1)}, u32[]{:S(2)}, u32[]{:S(2)}) %all-to-all-start) | async-done | bytes 65568 | tf_op jit(solution)/shard_map/all_to_all | solution.py:312
  31.2 2.6 %image.1 = (f32[64,64]{1,0:T(8,128)}, f32[64,64]{1,0:T(8,128)}) custom-call(bf16[256,128]{1,0:T(8,128)(2,1)S(1)} %bitcast.9, bf16[512,2816]{1,0:T(8,128)(2,1)S(1)} %get-tuple-element.10.cols_ref, f32[2,88,128]{2,1,0:T(8,128)S(1)} %get-tuple-element.11.aux_ref), custom_call_target="tpu_custom_call" | custom-call | flops 1476395008 | bytes 4194304 | tf_op jit(solution)/shard_map/image/pallas_call | solution.py:279
Async XLA Ops:
  2.8 28.4 %all-to-all-start = ((bf16[32,8,128]{2,1,0:T(8,128)(2,1)}), bf16[32,8,128]{2,1,0:T(8,128)(2,1)S(1)}, u32[]{:S(2)}, u32[]{:S(2)}) async-start(bf16[32,8,128]{2,1,0:T(8,128)(2,1)} %pack.1), calls=%async_computation | async-start | bytes 131072 | tf_op jit(solution)/shard_map/all_to_all | solution.py:312
  19.7 4.5 %collective-permute-start = (bf16[48,128]{1,0:T(8,128)(2,1)S(1)}, bf16[48,128]{1,0:T(8,128)(2,1)S(1)}, u32[]{:S(2)}, u32[]{:S(2)}) collective-permute-start(bf16[48,128]{1,0:T(8,128)(2,1)S(1)} %get-tuple-element.8), channel_id=1, source_target_pairs={{0,32},{64,96},{128,160},{192,224},{256,288},{320,352},{384,416},{... | collective-permute-start | bytes 36872 | tf_op jit(solution)/shard_map/ppermute | solution.py:316
  21.7 5.0 %collective-permute-start.1 = (bf16[48,128]{1,0:T(8,128)(2,1)S(1)}, bf16[48,128]{1,0:T(8,128)(2,1)S(1)}, u32[]{:S(2)}, u32[]{:S(2)}) collective-permute-start(bf16[48,128]{1,0:T(8,128)(2,1)S(1)} %get-tuple-element.9), channel_id=1, source_target_pairs={{32,64},{96,128},{160,192},{224,256},{288,320},{352,384},{416,448}... | collective-permute-start | bytes 36872 | tf_op jit(solution)/shard_map/ppermute | solution.py:316

commit v5 on v4

--- a/solution.py
+++ b/solution.py
@@ -191,7 +191,7 @@
     )(tile, kern, own, near, far)
 
 
-def image_kernel(taps_ref, cols_ref, aux_ref, grad_out, resist_out, grad_ref, resist_ref, done, wide, matrix, turned, fields, adjoint, sums, seen, final):
+def image_kernel(taps_ref, cols_ref, aux_ref, grad_ref, resist_ref, wide, matrix, turned, fields, adjoint, sums, seen, final):
     f32 = jnp.float32
     wide[...] = taps_ref[...].astype(f32)
     base = jnp.concatenate([wide[pl.ds(q, CHANNELS, stride=4), :] for q in range(4)], axis=1)
@@ -262,16 +262,9 @@
             spread_of(step - 2)
         if 0 <= step - 1 < CHUNKS:
             adjoint_of(step - 1)
-        if step == CHUNKS:
-            resist_ref[...] = pltpu.roll(seen[10:74, :], 118, 1)[:, :OWN]
-            resist_copy = pltpu.make_async_copy(resist_ref, resist_out, done.at[0])
-            resist_copy.start()
     grad = final[0, 4:68, :] + final[1, 0:64, :]
     grad_ref[...] = pltpu.roll(grad, 108, 1)[:, :OWN]
-    grad_copy = pltpu.make_async_copy(grad_ref, grad_out, done.at[1])
-    grad_copy.start()
-    resist_copy.wait()
-    grad_copy.wait()
+    resist_ref[...] = pltpu.roll(seen[10:74, :], 118, 1)[:, :OWN]
 
 
 def image(taps, cols, aux):
@@ -283,11 +276,8 @@
             jax.ShapeDtypeStruct((OWN, OWN), jnp.float32),
         ],
         in_specs=[pl.BlockSpec(memory_space=VMEM)] * 3,
-        out_specs=[pl.BlockSpec(memory_space=pl.ANY)] * 2,
+        out_specs=[pl.BlockSpec(memory_space=VMEM)] * 2,
         scratch_shapes=[
-            VMEM((OWN, OWN), jnp.float32),
-            VMEM((OWN, OWN), jnp.float32),
-            pltpu.SemaphoreType.DMA((2,)),
             VMEM((8 * SOURCES, 128), jnp.float32),
             VMEM((4 * CHANNELS, TAPS), jnp.bfloat16),
             VMEM((3 * BAND, 4 * CHANNELS), jnp.bfloat16),

time: 34.1 us -> 34.1 us (level)
  no operation moved by 1% of the time
where the time goes in v5:
time: 34.1 us; the launch traced here: 33.8 us
  starting transfers between devices  20.4 us (60%)
  waiting for transfers between devices  6.52 us (19%)
  Pallas kernels  5.51 us (16%)
  between operations  1.33 us (4%)
    all_to_all x1, starting transfers between devices, on_device(): taps = lax.all_to_all(sent, 'kern', split_axis=0, concat_axis=0, tiled=True)  16 us
    ppermute x2, starting transfers between devices, swapped(): return lax.ppermute(part, 'tile', pairs + [(j, i) for i, j in pairs])  4.47 us
    all_to_all x1, waiting for transfers between devices, on_device(): taps = lax.all_to_all(sent, 'kern', split_axis=0, concat_axis=0, tiled=True)  4.07 us
    pallas_call x1, Pallas kernels, image(): pl.pallas_call(image_kernel, out_shape=[jax.ShapeDtypeStruct((OWN, OWN),...  2.59 us
    ppermute x2, waiting for transfers between devices, swapped(): return lax.ppermute(part, 'tile', pairs + [(j, i) for i, j in pairs])  2.45 us
    pallas_call x1, Pallas kernels, pack(): pl.pallas_call(pack_kernel, out_shape=jax.ShapeDtypeStruct((SOURCES, 8, 1...  1.52 us
    pallas_call x1, Pallas kernels, window(): pl.pallas_call(window_kernel, grid_spec=pltpu.PrefetchScalarGridSpec(num_...  0.95 us
  transfers between devices with their start and end apart: 3, of which 2 were waited for; matrix products, arithmetic and copies ran while one was open for 0% of the time, Pallas kernels for 4%

profile of v5, /device:TPU:2, one launch (start us, length us, event | category | flops | bytes accessed | tf_op | source)
XLA Modules:
  0.0 33.8 jit_solution(4488578658847174038)
XLA Ops:
  1.3 1.5 %pack.1 = bf16[32,8,128]{2,1,0:T(8,128)(2,1)} custom-call(s32[1,1]{1,0:T(1,128)} %bitcast.8.assign_ref, bf16[21,2,21]{2,1,0:T(2,128)(2,1)} %bitcast.10, f32[1,32]{1,0:T(1,128)} %bitcast.11), custom_call_target="tpu_custom_call" | custom-call | tf_op jit(solution)/shard_map/pack/pallas_call | solution.py:56
  2.8 16.0 %all-to-all-start = ((bf16[32,8,128]{2,1,0:T(8,128)(2,1)}), bf16[32,8,128]{2,1,0:T(8,128)(2,1)S(1)}, u32[]{:S(2)}, u32[]{:S(2)}) async-start(bf16[32,8,128]{2,1,0:T(8,128)(2,1)} %pack.1), calls=%async_computation | async-start | bytes 131072 | tf_op jit(solution)/shard_map/all_to_all | solution.py:302
  18.8 1.0 %window.1 = (bf16[128,128]{1,0:T(8,128)(2,1)S(1)}, bf16[48,128]{1,0:T(8,128)(2,1)S(1)}, bf16[48,128]{1,0:T(8,128)(2,1)S(1)}) custom-call(s32[1]{0:T(128)} %bitcast.5.tile_ref, s32[1]{0:T(128)} %bitcast.6.kern_ref, f32[64,2048]{1,0:T(8,128)} %mask_b.1, f32[64,2048]{1,0:T(8,128)} %mask_b.1, s32[64,2048]{1,0:T(8,128)} %target_b.1, s32[64,2048]{1,0:T(8,128)} %target_b.1), custom_call_target="tpu_custom_call" | custom-call | tf_op jit(solution)/shard_map/window/pallas_call | solution.py:107
  19.7 1.9 %collective-permute-start = (bf16[48,128]{1,0:T(8,128)(2,1)S(1)}, bf16[48,128]{1,0:T(8,128)(2,1)S(1)}, u32[]{:S(2)}, u32[]{:S(2)}) collective-permute-start(bf16[48,128]{1,0:T(8,128)(2,1)S(1)} %get-tuple-element.8), channel_id=1, source_target_pairs={{0,32},{64,96},{128,160},{192,224},{256,288},{320,352},{384,416},{... | collective-permute-start | bytes 36872 | tf_op jit(solution)/shard_map/ppermute | solution.py:306
  21.7 2.5 %collective-permute-start.1 = (bf16[48,128]{1,0:T(8,128)(2,1)S(1)}, bf16[48,128]{1,0:T(8,128)(2,1)S(1)}, u32[]{:S(2)}, u32[]{:S(2)}) collective-permute-start(bf16[48,128]{1,0:T(8,128)(2,1)S(1)} %get-tuple-element.9), channel_id=1, source_target_pairs={{32,64},{96,128},{160,192},{224,256},{288,320},{352,384},{416,448}... | collective-permute-start | bytes 36872 | tf_op jit(solution)/shard_map/ppermute | solution.py:306
  24.2 0.0 collective-permute-done.near_ref
  24.2 2.5 %collective-permute-done.1.far_ref = bf16[48,128]{1,0:T(8,128)(2,1)S(1)} collective-permute-done((bf16[48,128]{1,0:T(8,128)(2,1)S(1)}, bf16[48,128]{1,0:T(8,128)(2,1)S(1)}, u32[]{:S(2)}, u32[]{:S(2)}) %collective-permute-start.1) | collective-permute-done | bytes 12320 | tf_op jit(solution)/shard_map/ppermute | solution.py:306
  26.7 0.4 %columns.1 = (bf16[512,2816]{1,0:T(8,128)(2,1)S(1)}, f32[2,88,128]{2,1,0:T(8,128)S(1)}) custom-call(s32[1]{0:T(128)} %bitcast.5.tile_ref, s32[1]{0:T(128)} %bitcast.6.kern_ref, bf16[128,128]{1,0:T(8,128)(2,1)S(1)} %get-tuple-element.7.own_ref, bf16[48,128]{1,0:T(8,128)(2,1)S(1)} %collective-permute-done.near_ref, ...), custom_call_target="tpu_custom_call" | custom-call | flops 1048576 | bytes 4194304 | tf_op jit(solution)/shard_map/columns/pallas_call | solution.py:179
  27.1 4.1 %all-to-all-done = bf16[32,8,128]{2,1,0:T(8,128)(2,1)S(1)} async-done(((bf16[32,8,128]{2,1,0:T(8,128)(2,1)}), bf16[32,8,128]{2,1,0:T(8,128)(2,1)S(1)}, u32[]{:S(2)}, u32[]{:S(2)}) %all-to-all-start) | async-done | bytes 65568 | tf_op jit(solution)/shard_map/all_to_all | solution.py:302
  31.2 2.6 %image.1 = (f32[64,64]{1,0:T(8,128)}, f32[64,64]{1,0:T(8,128)}) custom-call(bf16[256,128]{1,0:T(8,128)(2,1)S(1)} %bitcast.9, bf16[512,2816]{1,0:T(8,128)(2,1)S(1)} %get-tuple-element.10.cols_ref, f32[2,88,128]{2,1,0:T(8,128)S(1)} %get-tuple-element.11.aux_ref), custom_call_target="tpu_custom_call" | custom-call | flops 1476395008 | bytes 4194304 | tf_op jit(solution)/shard_map/image/pallas_call | solution.py:272
Async XLA Ops:
  2.8 28.4 %all-to-all-start = ((bf16[32,8,128]{2,1,0:T(8,128)(2,1)}), bf16[32,8,128]{2,1,0:T(8,128)(2,1)S(1)}, u32[]{:S(2)}, u32[]{:S(2)}) async-start(bf16[32,8,128]{2,1,0:T(8,128)(2,1)} %pack.1), calls=%async_computation | async-start | bytes 131072 | tf_op jit(solution)/shard_map/all_to_all | solution.py:302
  19.7 4.5 %collective-permute-start = (bf16[48,128]{1,0:T(8,128)(2,1)S(1)}, bf16[48,128]{1,0:T(8,128)(2,1)S(1)}, u32[]{:S(2)}, u32[]{:S(2)}) collective-permute-start(bf16[48,128]{1,0:T(8,128)(2,1)S(1)} %get-tuple-element.8), channel_id=1, source_target_pairs={{0,32},{64,96},{128,160},{192,224},{256,288},{320,352},{384,416},{... | collective-permute-start | bytes 36872 | tf_op jit(solution)/shard_map/ppermute | solution.py:306
  21.7 5.0 %collective-permute-start.1 = (bf16[48,128]{1,0:T(8,128)(2,1)S(1)}, bf16[48,128]{1,0:T(8,128)(2,1)S(1)}, u32[]{:S(2)}, u32[]{:S(2)}) collective-permute-start(bf16[48,128]{1,0:T(8,128)(2,1)S(1)} %get-tuple-element.9), channel_id=1, source_target_pairs={{32,64},{96,128},{160,192},{224,256},{288,320},{352,384},{416,448}... | collective-permute-start | bytes 36872 | tf_op jit(solution)/shard_map/ppermute | solution.py:306
